TPU v7x, 32 devices: a whole 2x2x4 slice. The times are simulated.
32 devices in a mesh: pipe: 4 (over z), expert: 8 (over y, x, core).
Axes of the slice: x: 2, y: 2, z: 4, core: 2. Of those that a mesh axis runs over, the one named last changes fastest.
Arguments:
- fwd_state: bfloat16 [4, 192, 3584], P('pipe', 'expert'), may hold values from -6 to 6
- bwd_state: bfloat16 [4, 192, 3584], P('pipe', 'expert'), may hold values from -6 to 6
- saved_input: bfloat16 [4, 2, 192, 3584], P('pipe', None, 'expert'), may hold values from -6 to 6
- fwd_route: int32 [4, 2, 192, 1], P('pipe', None, 'expert'), may hold values from 0 to 3; in each aligned block of 24 rows (0 to 23, 24 to 47, ..., all dimensions but the last counted through in order) at most 7 rows name the same one
- bwd_route: int32 [4, 2, 192, 1], P('pipe', None, 'expert'), may hold values from 0 to 3; in each aligned block of 24 rows (0 to 23, 24 to 47, ..., all dimensions but the last counted through in order) at most 7 rows name the same one
- fwd_gate: float32 [4, 2, 192], P('pipe', None, 'expert'), may hold values from 0.3 to 1
- bwd_gate: float32 [4, 2, 192], P('pipe', None, 'expert'), may hold values from 0.3 to 1
- w_gate: bfloat16 [4, 3584, 1024], P('pipe', None, 'expert'), may hold values from -0.09375 to 0.09375
- w_up: bfloat16 [4, 3584, 1024], P('pipe', None, 'expert'), may hold values from -0.09375 to 0.09375
- w_down: bfloat16 [4, 1024, 3584], P('pipe', 'expert'), may hold values from -0.375 to 0.375
- norm_gain: float32 [4, 3584], P('pipe'), may hold values from 0.5 to 1.5
Outputs:
- fwd_out: bfloat16 [4, 192, 3584], P('pipe', 'expert')
- bwd_out: bfloat16 [4, 192, 3584], P('pipe', 'expert')
Inputs may be any that keep to these rules, and one draw needn't show every extreme that they name: `fwd_route`: in the rows of one device at one rank and step, no expert is named more than 7 times, and one is named exactly 7 times. `bwd_route`: as for fwd_route.
All inputs are finite; a program needn't handle non-finite values.
Results may differ from a plain program's by a relative error of at most 0.0068.
Values may be sent and summed in bfloat16 or wider, within the bound.
No kernel may reach another device: no remote copies, remote signals or barrier semaphores. Data moves between devices by JAX's collectives and lax.ppermute only.
A program may use at most 64 MiB of HBM per device.

v0:
```python
import functools

import jax
import jax.numpy as jnp
from jax import lax
from jax.experimental import pallas as pl
from jax.experimental.pallas import tpu as pltpu
from jax.sharding import PartitionSpec as P

EXPERTS = 4
CAP = 7
EPS = 1e-06


SLOT = -(-CAP // 8) * 8
LANES = 128
F32 = jnp.float32
BF16 = jnp.bfloat16


def call(body, outs, args, vmem=16, **more):
    return pl.pallas_call(
        body,
        out_shape=outs,
        compiler_params=pltpu.CompilerParams(vmem_limit_bytes=vmem * 2**20),
        **more,
    )(*args)


def place():
    device = lax.axis_index("expert")
    return device // 2, device % 2


def swap_cores(array):
    pairs = [(i, i ^ 1) for i in range(lax.axis_size("expert"))]
    return lax.ppermute(array, "expert", pairs)


def exchange(pieces):
    moved = [pieces[0]]
    for m in range(1, EXPERTS):
        pairs = [(i, i ^ (2 * m)) for i in range(lax.axis_size("expert"))]
        moved.append(lax.ppermute(pieces[m], "expert", pairs))
    return moved


def swap_ranks(array, first):
    ranks_total, devices = lax.axis_size("pipe"), lax.axis_size("expert")
    target = [i ^ 1 for i in range(ranks_total * devices)]
    for rank in range(first, ranks_total - 1, 2):
        for i in range(devices):
            a, b = rank * devices + i, (rank + 1) * devices + i
            target[a], target[b] = b, a
    return lax.ppermute(array, ("pipe", "expert"), list(enumerate(target)))


def slot_hits(routes):
    count, tokens = routes.shape
    chip, _ = place()
    routes = routes.astype(jnp.int32)
    expert = lax.broadcasted_iota(jnp.int32, (EXPERTS, tokens), 0)
    named = [jnp.where(expert == routes[i : i + 1], 1.0, 0.0) for i in range(count)]
    down = lax.broadcasted_iota(jnp.int32, (tokens, tokens), 0)
    across = lax.broadcasted_iota(jnp.int32, (tokens, tokens), 1)
    earlier = jnp.where(down < across, 1.0, 0.0).astype(BF16)
    stacked = jnp.concatenate(named, axis=0)
    before = placed(stacked.astype(BF16), earlier) * stacked
    slot = lax.broadcasted_iota(jnp.int32, (EXPERTS * SLOT, tokens), 0)
    hits = []
    for i in range(count):
        rank = jnp.sum(before[i * EXPERTS : (i + 1) * EXPERTS], axis=0, keepdims=True)
        hits.append(slot == (routes[i : i + 1] ^ chip) * SLOT + rank.astype(jnp.int32))
    return hits


def as_table(hits):
    return jnp.where(hits, 1.0, 0.0)


def slot_gates(fwd_hits, bwd_hits, fwd_gates, bwd_gates):
    lane = lax.broadcasted_iota(jnp.int32, (EXPERTS * SLOT, LANES), 1)
    value = jnp.zeros(lane.shape, F32)
    for i, (hits, gates) in enumerate(((fwd_hits, fwd_gates), (bwd_hits, bwd_gates))):
        gate = jnp.sum(jnp.where(hits, gates, 0.0), axis=1, keepdims=True)
        high = gate.astype(BF16).astype(F32)
        value = jnp.where(lane == 2 * i, high, jnp.where(lane == 2 * i + 1, gate - high, value))
    return value


def placed(table, rows):
    return jnp.dot(table, rows, preferred_element_type=F32)


def put_pieces(outs, at, value):
    for m, out in enumerate(outs):
        out[:, at : at + value.shape[1]] = value[m * SLOT : (m + 1) * SLOT].astype(BF16)


def folded(width):
    if SLOT == CAP:
        return width, 0
    tail = width // LANES // (CAP + 1) * LANES
    return width - tail, tail


def put_folded(outs, at, parts):
    head, tail = folded(sum(p.shape[1] for p in parts))
    down = lax.broadcasted_iota(jnp.int32, (SLOT, head), 0)
    for m, out in enumerate(outs):
        rows = jnp.concatenate([p[m * SLOT : (m + 1) * SLOT] for p in parts], axis=1)
        value = rows[:, :head]
        if tail:
            ends = [jnp.broadcast_to(rows[r : r + 1, head:], (SLOT, tail)) for r in range(CAP)]
            if head > CAP * tail:
                ends.append(jnp.zeros((SLOT, head - CAP * tail), F32))
            value = jnp.where(down == CAP, jnp.concatenate(ends, axis=1), value)
        out[:, at : at + head] = value.astype(BF16)


def unfolded(pieces, at, width):
    head, tail = folded(width)
    main = jnp.concatenate([p[:, at : at + head] for p in pieces], axis=0)
    if not tail:
        return main
    down = lax.broadcasted_iota(jnp.int32, (SLOT, tail), 0)
    ends = []
    for p in pieces:
        row = p[:, at : at + CAP * tail].astype(F32)[CAP : CAP + 1]
        end = jnp.zeros((SLOT, tail), F32)
        for r in range(CAP):
            end = jnp.where(down == r, row[:, r * tail : (r + 1) * tail], end)
        ends.append(end)
    return jnp.concatenate([main, jnp.concatenate(ends, axis=0).astype(BF16)], axis=1)


def first_spread_body(steps, tokens, *refs):
    small, (state, grad, saved), refs = refs[:4], refs[4:7], refs[7:]
    lines, outs, scratch, sems = refs[0], refs[1 : 1 + EXPERTS], refs[1 + EXPERTS : -1], refs[-1]
    sources = [*small, state, grad, saved.at[pl.ds(0, tokens), :]]
    copies = [
        pltpu.make_async_copy(src, dst, sems.at[i])
        for i, (src, dst) in enumerate(zip(sources, scratch))
    ]
    for copy in copies:
        copy.start()
    lines[...] = jnp.zeros(lines.shape, F32)
    for i in range(4):
        copies[i].wait()
        lines[i * steps : (i + 1) * steps, :tokens] = scratch[i][...].astype(F32)
    routes = jnp.concatenate([scratch[0][0:1], scratch[1][0:1]], axis=0)
    fwd_hits, bwd_hits = slot_hits(routes)
    put_pieces(outs, 0, slot_gates(fwd_hits, bwd_hits, scratch[2][0:1], scratch[3][0:1]))
    fwd_table, bwd_table = as_table(fwd_hits).astype(BF16), as_table(bwd_hits).astype(BF16)
    parts = []
    for i, table in enumerate((fwd_table, bwd_table, bwd_table)):
        copies[4 + i].wait()
        parts.append(placed(table, scratch[4 + i][...]))
    put_folded(outs, LANES, parts)


def first_spread(small, state, grad, saved):
    steps, tokens = small[0].shape
    width = state.shape[1]
    outs = [jax.ShapeDtypeStruct((-(-4 * steps // 8) * 8, LANES), F32)]
    outs += [jax.ShapeDtypeStruct((SLOT, LANES + folded(3 * width)[0]), BF16)] * EXPERTS
    args = [*small, state, grad, saved]
    return call(
        functools.partial(first_spread_body, steps, tokens),
        outs,
        [pltpu.with_memory_space_constraint(a, pltpu.HBM) for a in args],
        in_specs=[pl.BlockSpec(memory_space=pltpu.HBM)] * len(args),
        scratch_shapes=[pltpu.VMEM((steps, tokens), a.dtype) for a in small]
        + [pltpu.VMEM((tokens, width), BF16)] * 3
        + [pltpu.SemaphoreType.DMA((len(args),))],
    )


def prepare_body(steps, tokens, *refs):
    lines, saved, to_tokens, to_slots, gates, later = *refs[:5], refs[5:]
    rank, last = lax.axis_index("pipe"), lax.axis_size("pipe") - 1
    rows = lines[...]
    across = slice(0, tokens)
    for step in range(steps):
        at = (step, steps + step, 2 * steps + step, 3 * steps + step)
        fwd_row, bwd_row, fwd_gate, bwd_gate = (rows[i : i + 1, across] for i in at)
        hits = slot_hits(jnp.concatenate([fwd_row, bwd_row], axis=0))
        gates[step] = slot_gates(*hits, fwd_gate, bwd_gate).astype(BF16)
        for i, end in enumerate((0, last)):
            table = as_table(hits[i])
            to_tokens[2 * step + i] = table.T.astype(BF16)
            come = as_table(hits[i] & (rank != end)).astype(BF16)
            to_slots[2 * step + i] = come
        if step:
            table = table.astype(BF16)
            outs = later[(step - 1) * EXPERTS : step * EXPERTS]
            put_pieces(outs, 0, placed(table, saved[step * tokens : (step + 1) * tokens, :]))


def prepare(lines, saved, steps, tokens):
    slots = EXPERTS * SLOT
    outs = [
        jax.ShapeDtypeStruct((2 * steps, tokens, slots), BF16),
        jax.ShapeDtypeStruct((2 * steps, slots, tokens), BF16),
        jax.ShapeDtypeStruct((steps, slots, LANES), BF16),
    ]
    outs += [jax.ShapeDtypeStruct((SLOT, saved.shape[1]), BF16)] * (EXPERTS * (steps - 1))
    body = functools.partial(prepare_body, steps, tokens)
    to_tokens, to_slots, gates, *later = call(body, outs, [lines, saved])
    later = [later[i * EXPERTS : (i + 1) * EXPERTS] for i in range(steps - 1)]
    return (to_tokens, to_slots, gates), later


def spread_body(step, tables, gates, low, high, *outs):
    even = lax.axis_index("pipe") % 2 == 0
    for m, out in enumerate(outs):
        out[:, :LANES] = gates[step, m * SLOT : (m + 1) * SLOT, :]

    def put(forward, backward):
        parts = [
            placed(tables[2 * step + i], rows[...]) for i, rows in enumerate((forward, backward))
        ]
        put_folded(outs, LANES, parts)

    pl.when(even)(lambda: put(high, low))
    pl.when(jnp.logical_not(even))(lambda: put(low, high))


def gather_body(step, last, tables, *refs):
    pieces, outs = refs[:EXPERTS], refs[EXPERTS:]
    width = outs[0].shape[1]

    slots = unfolded(pieces, 0, 2 * width)

    def put(*targets):
        for stream, out in enumerate(targets):
            rows = slots[:, stream * width : (stream + 1) * width]
            out[...] = placed(tables[2 * step + stream], rows).astype(BF16)

    if last:
        put(*outs)
    else:
        even = lax.axis_index("pipe") % 2 == 0
        pl.when(even)(lambda: put(outs[0], outs[1]))
        pl.when(jnp.logical_not(even))(lambda: put(outs[1], outs[0]))


def weight_targets(outs, j, h):
    _, core = place()
    cols_out, rows_out = outs[:2]
    at = pl.multiple_of((core ^ j) * h, h)
    return (
        cols_out.at[:, pl.ds(at, h)],
        cols_out.at[:, pl.ds(pl.multiple_of(2 * h + at, h), h)],
        rows_out.at[pl.ds(at, h), :],
    )


def flip_weights(outs, j, h):
    _, core = place()
    cols_flip, rows_flip = outs[2:]
    at = pl.multiple_of((core ^ j) * h, h)
    gates, ups, downs = weight_targets(outs, j, h)
    cols_flip[pl.ds(at, h), :] = gates[...].T
    cols_flip[pl.ds(pl.multiple_of(2 * h + at, h), h), :] = ups[...].T
    rows_flip[:, pl.ds(at, h)] = downs[...].T


def pack_own_body(*refs):
    own, outs, sems = refs[:3], refs[3:7], refs[7]
    h = own[0].shape[1]
    copies = [
        pltpu.make_async_copy(src, dst, sems.at[i])
        for i, (src, dst) in enumerate(zip(own, weight_targets(outs, 0, h)))
    ]
    for copy in copies:
        copy.start()
    for copy in copies:
        copy.wait()
    flip_weights(outs, 0, h)


def pack_other_body(*refs):
    other, outs = refs[:3], refs[7:]
    h = other[0].shape[1]
    for src, dst in zip(other, weight_targets(outs, 1, h)):
        dst[...] = src[...]
    flip_weights(outs, 1, h)


def pack(own):
    width, units = own[0].shape
    shapes = ((width, 4 * units), (2 * units, width), (4 * units, width), (width, 2 * units))
    outs = [jax.ShapeDtypeStruct(shape, BF16) for shape in shapes]
    others = [swap_cores(array) for array in own]
    begun = call(
        pack_own_body,
        outs,
        [pltpu.with_memory_space_constraint(array, pltpu.HBM) for array in own],
        in_specs=[pl.BlockSpec(memory_space=pltpu.HBM)] * 3,
        scratch_shapes=[pltpu.SemaphoreType.DMA((3,))],
    )
    return call(
        pack_other_body,
        outs,
        [*others, *begun],
        in_specs=[pl.BlockSpec(memory_space=pltpu.VMEM)] * 7,
        input_output_aliases={3 + i: i for i in range(4)},
    )


def normed_of(rows, gain_ref):
    values = rows.astype(F32)
    mean = jnp.mean(values * values, axis=-1, keepdims=True)
    scale = lax.rsqrt(mean + EPS)
    return scale, (values * scale * gain_ref[...]).astype(BF16)


def expert_body(gain_ref, cols_ref, rows_ref, cols_flip, rows_flip, *refs):
    pieces, outs = refs[:EXPERTS], refs[len(refs) - EXPERTS :]
    n, width = rows_ref.shape
    half = EXPERTS * SLOT

    gates = jnp.concatenate([p[:, :LANES] for p in pieces], axis=0).astype(F32)
    if len(refs) == 2 * EXPERTS:
        slots = unfolded(pieces, LANES, 3 * width)
        saved = slots[:, 2 * width :]
    else:
        slots = unfolded(pieces, LANES, 2 * width)
        saved = jnp.concatenate([p[...] for p in refs[EXPERTS : 2 * EXPERTS]], axis=0)
    state, grad = slots[:, :width], slots[:, width : 2 * width]
    dhidden = jnp.dot(grad, rows_flip[...], preferred_element_type=F32)
    dhidden = dhidden * (gates[:, 2:3] + gates[:, 3:4])
    _, fwd_normed = normed_of(state, gain_ref)
    scale, bwd_normed = normed_of(saved, gain_ref)
    normed = jnp.concatenate([fwd_normed, bwd_normed], axis=0)
    both = jnp.dot(normed, cols_ref[...], preferred_element_type=F32)

    gated, upped = both[:half, :n], both[:half, n:]
    hidden = (gated * jax.nn.sigmoid(gated) * upped).astype(BF16)
    moe = jnp.dot(hidden, rows_ref[...], preferred_element_type=F32)
    new_state = state.astype(F32) + (gates[:, 0:1] + gates[:, 1:2]) * moe

    gated, upped = both[half:, :n], both[half:, n:]
    sigma = jax.nn.sigmoid(gated)
    dgate = (dhidden * upped * sigma * (1.0 + gated * (1.0 - sigma))).astype(BF16)
    dup = (dhidden * gated * sigma).astype(BF16)
    dnorm = jnp.dot(
        jnp.concatenate([dgate, dup], axis=1), cols_flip[...], preferred_element_type=F32
    )
    inner = dgate.astype(F32) * gated + dup.astype(F32) * upped
    mean = jnp.sum(inner, axis=-1, keepdims=True) / width
    value = grad.astype(F32) + scale * (gain_ref[...] * dnorm)
    put_folded(outs, 0, [new_state, value - saved.astype(F32) * (scale * scale * mean)])


def by_home_core(
    fwd_state,
    bwd_state,
    saved_input,
    fwd_route,
    bwd_route,
    fwd_gate,
    bwd_gate,
    w_gate,
    w_up,
    w_down,
    norm_gain,
):
    tokens, width = fwd_state.shape[1:]
    steps = fwd_route.shape[1]
    saved = saved_input[0].reshape(steps * tokens, width)
    small = [a.reshape(steps, tokens) for a in (fwd_route, bwd_route, fwd_gate, bwd_gate)]
    lines, *made = first_spread(small, fwd_state[0], bwd_state[0], saved)
    made, own = lax.optimization_barrier((made, (w_gate[0], w_up[0], w_down[0])))
    pieces = exchange(made)
    weights = pack(own)
    pair = folded(2 * width)[0]
    two = [jax.ShapeDtypeStruct((SLOT, pair), BF16)] * EXPERTS
    main = [jax.ShapeDtypeStruct((SLOT, LANES + pair), BF16)] * EXPERTS
    state = [jax.ShapeDtypeStruct((tokens, width), BF16)] * 2
    tables, later = prepare(lines, saved, steps, tokens)
    weights, tables, later = lax.optimization_barrier((weights, tables, later))
    to_tokens, to_slots, gates = tables
    for step in range(steps):
        back = call(expert_body, two, [norm_gain, *weights, *pieces])
        last = step + 1 == steps
        back = exchange(back)
        body = functools.partial(gather_body, step, last)
        made = call(body, state, [to_tokens, *back])
        if last:
            return made[0][None], made[1][None]
        made, ahead = lax.optimization_barrier((made, later[step]))
        high = swap_ranks(made[1], 1)
        low = swap_ranks(made[0], 0)
        ahead = exchange(ahead)
        body = functools.partial(spread_body, step + 1)
        made = call(body, main, [to_slots, gates, low, high])
        pieces = exchange(made) + ahead


def passed_along(array, axis, by):
    size = lax.axis_size(axis)
    pairs = [(i, i + by) for i in range(size) if 0 <= i + by < size]
    return lax.ppermute(array, axis, pairs)


def norm_rows(rows, gain):
    raw = rows.astype(jnp.float32)
    scale = lax.rsqrt(jnp.mean(raw * raw, axis=-1, keepdims=True) + EPS)
    return (raw, scale, (raw * scale * gain).astype(jnp.bfloat16))


def slot_index(route):
    hits = (route[:, None] == jnp.arange(EXPERTS, dtype=jnp.int32)[None, :]).astype(jnp.int32)
    before = jnp.cumsum(hits, axis=0) - hits
    return route * CAP + jnp.sum(before * hits, axis=1)


def slot_table(index):
    columns = jnp.arange(EXPERTS * CAP, dtype=jnp.int32)
    return (columns[:, None] == index[None, :]).astype(jnp.bfloat16)


def fill_slots(table, rows, shards):
    picked = jnp.dot(table, rows, preferred_element_type=jnp.float32).astype(jnp.bfloat16)
    return jnp.repeat(picked.reshape(EXPERTS, CAP, rows.shape[1]), shards, axis=0)


def collect_rows(returned, index, shards):
    width = returned.shape[2]
    summed = (
        returned.reshape(EXPERTS, shards, returned.shape[1], width).astype(jnp.float32).sum(axis=1)
    )
    return jnp.take(summed.reshape(EXPERTS * CAP, width), index, axis=0)


def by_all_to_all(
    fwd_state,
    bwd_state,
    saved_input,
    fwd_route,
    bwd_route,
    fwd_gate,
    bwd_gate,
    w_gate,
    w_up,
    w_down,
    norm_gain,
):
    shards = lax.axis_size("expert") // EXPERTS
    gain = norm_gain[0]
    gate_cols = w_gate[0]
    up_cols = w_up[0]
    down_rows = w_down[0]
    steps_total = fwd_route.shape[1]
    forward = fwd_state[0]
    backward = bwd_state[0]
    new_forward = forward
    new_backward = backward
    for moment in range(steps_total):
        fwd_index = slot_index(fwd_route[0, moment, :, 0])
        fwd_raw, _, fwd_norm = norm_rows(forward, gain)
        fwd_slots = fill_slots(slot_table(fwd_index), fwd_norm, shards)
        bwd_index = slot_index(bwd_route[0, moment, :, 0])
        bwd_table = slot_table(bwd_index)
        bwd_raw, bwd_scale, bwd_norm = norm_rows(saved_input[0, moment], gain)
        scaled = (bwd_gate[0, moment][:, None] * backward.astype(jnp.float32)).astype(jnp.bfloat16)
        bwd_inputs = fill_slots(bwd_table, bwd_norm, shards)
        bwd_grads = fill_slots(bwd_table, scaled, shards)
        expert_received = lax.all_to_all(
            fwd_slots, "expert", split_axis=0, concat_axis=0, tiled=True
        )
        expert_gated = jnp.einsum(
            "scd,dh->sch", expert_received, gate_cols, preferred_element_type=jnp.float32
        )
        expert_upped = jnp.einsum(
            "scd,dh->sch", expert_received, up_cols, preferred_element_type=jnp.float32
        )
        hidden = (expert_gated * jax.nn.sigmoid(expert_gated) * expert_upped).astype(jnp.bfloat16)
        fwd_partial = jnp.einsum(
            "sch,hd->scd", hidden, down_rows, preferred_element_type=jnp.float32
        ).astype(jnp.bfloat16)
        fwd_back = lax.all_to_all(fwd_partial, "expert", split_axis=0, concat_axis=0, tiled=True)
        inputs_part = lax.all_to_all(bwd_inputs, "expert", split_axis=0, concat_axis=0, tiled=True)
        grads_part = lax.all_to_all(bwd_grads, "expert", split_axis=0, concat_axis=0, tiled=True)
        gated = jnp.einsum(
            "scd,dh->sch", inputs_part, gate_cols, preferred_element_type=jnp.float32
        )
        upped = jnp.einsum("scd,dh->sch", inputs_part, up_cols, preferred_element_type=jnp.float32)
        dhidden = jnp.einsum(
            "scd,hd->sch", grads_part, down_rows, preferred_element_type=jnp.float32
        )
        sigma = jax.nn.sigmoid(gated)
        dgate = (dhidden * upped * sigma * (1.0 + gated * (1.0 - sigma))).astype(jnp.bfloat16)
        dup = (dhidden * gated * sigma).astype(jnp.bfloat16)
        result = jnp.einsum("sch,dh->scd", dgate, gate_cols, preferred_element_type=jnp.float32)
        result = result + jnp.einsum(
            "sch,dh->scd", dup, up_cols, preferred_element_type=jnp.float32
        )
        bwd_partial = result.astype(jnp.bfloat16)
        bwd_back = lax.all_to_all(bwd_partial, "expert", split_axis=0, concat_axis=0, tiled=True)
        moe_rows = collect_rows(fwd_back, fwd_index, shards)
        new_forward = (fwd_raw + fwd_gate[0, moment][:, None] * moe_rows).astype(jnp.bfloat16)
        dnorm = collect_rows(bwd_back, bwd_index, shards)
        weighted = gain * dnorm
        cubed = bwd_scale * bwd_scale * bwd_scale
        dinput = bwd_scale * weighted - bwd_raw * cubed * jnp.mean(
            bwd_raw * weighted, axis=-1, keepdims=True
        )
        new_backward = (backward.astype(jnp.float32) + dinput).astype(jnp.bfloat16)
        if moment + 1 < steps_total:
            forward = passed_along(new_forward, "pipe", 1)
            backward = passed_along(new_backward, "pipe", -1)
    return (new_forward[None], new_backward[None])


def local(*args):
    if lax.axis_size("expert") == 2 * EXPERTS:
        return by_home_core(*args)
    return by_all_to_all(*args)


def solution(mesh):
    specs = (
        P("pipe", "expert", None),
        P("pipe", "expert", None),
        P("pipe", None, "expert", None),
        P("pipe", None, "expert", None),
        P("pipe", None, "expert", None),
        P("pipe", None, "expert"),
        P("pipe", None, "expert"),
        P("pipe", None, "expert"),
        P("pipe", None, "expert"),
        P("pipe", "expert", None),
        P("pipe", None),
    )
    return jax.shard_map(
        local,
        mesh=mesh,
        in_specs=specs,
        out_specs=(P("pipe", "expert", None), P("pipe", "expert", None)),
        check_vma=False,
    )
```

profile of v0, /device:TPU:0, one launch (start us, length us, event | category | flops | bytes accessed | tf_op | source)
XLA Modules:
  0.0 54.1 jit_solution(17004297667517000182)
XLA Ops:
  0.6 0.0 copy-start
  0.6 1.8 %shard_map.122 = (f32[8,128]{1,0:T(8,128)S(1)}, bf16[8,9600]{1,0:T(8,128)(2,1)S(1)}, bf16[8,9600]{1,0:T(8,128)(2,1)S(1)}, bf16[8,9600]{1,0:T(8,128)(2,1)S(1)}, bf16[8,9600]{1,0:T(8,128)(2,1)S(1)}) custom-call(s32[2,24]{1,0:T(2,128)} %bitcast.22, s32[2,24]{1,0:T(2,128)} %bitcast.23, f32[2,24]{1,0:T(2,128)} %bitcast.24, f32[2,24]{1,0:T(2,128)} %bitcast.25, ...), custom_call_target="tpu_custom_call" | custom-call | tf_op jit(solution)/shard_map/pallas_call | solution.py:22
  2.4 0.6 %collective-permute-start = (bf16[3584,128]{1,0:T(8,128)(2,1)}, bf16[3584,128]{1,0:T(8,128)(2,1)S(1)}, u32[]{:S(2)}, u32[]{:S(2)}) collective-permute-start(bf16[3584,128]{1,0:T(8,128)(2,1)} %bitcast.14), channel_id=1, source_target_pairs={{0,1},{1,0},{2,3},{3,2},{4,5},{5,4},{6,7},{7,6},{8,9},{9,8},{10,11... | collective-permute-start | bytes 2752520 | tf_op jit(solution)/shard_map/ppermute | solution.py:37
  3.0 0.1 collective-permute-start.1
  3.0 0.4 collective-permute-start.2
  3.5 2.6 %collective-permute-start.3 = (bf16[8,9600]{1,0:T(8,128)(2,1)S(1)}, bf16[8,9600]{1,0:T(8,128)(2,1)S(1)}, u32[]{:S(2)}, u32[]{:S(2)}) collective-permute-start(bf16[8,9600]{1,0:T(8,128)(2,1)S(1)} %get-tuple-element.93), channel_id=1, source_target_pairs={{0,2},{1,3},{2,0},{3,1},{4,6},{5,7},{6,4},{7,5},{8,10},{9,11},{10,... | collective-permute-start | bytes 460808 | tf_op jit(solution)/shard_map/ppermute | solution.py:44
  6.0 1.5 %collective-permute-start.4 = (bf16[8,9600]{1,0:T(8,128)(2,1)S(1)}, bf16[8,9600]{1,0:T(8,128)(2,1)S(1)}, u32[]{:S(2)}, u32[]{:S(2)}) collective-permute-start(bf16[8,9600]{1,0:T(8,128)(2,1)S(1)} %get-tuple-element.94), channel_id=1, source_target_pairs={{0,4},{1,5},{2,6},{3,7},{4,0},{5,1},{6,2},{7,3},{8,12},{9,13},{10,... | collective-permute-start | bytes 460808 | tf_op jit(solution)/shard_map/ppermute | solution.py:44
  7.6 0.0 collective-permute-done.refs_0_
  7.6 1.5 %collective-permute-start.5 = (bf16[8,9600]{1,0:T(8,128)(2,1)S(1)}, bf16[8,9600]{1,0:T(8,128)(2,1)S(1)}, u32[]{:S(2)}, u32[]{:S(2)}) collective-permute-start(bf16[8,9600]{1,0:T(8,128)(2,1)S(1)} %get-tuple-element.95), channel_id=1, source_target_pairs={{0,6},{1,7},{2,4},{3,5},{4,2},{5,3},{6,0},{7,1},{8,14},{9,15},{10,... | collective-permute-start | bytes 460808 | tf_op jit(solution)/shard_map/ppermute | solution.py:44
  9.1 2.5 %shard_map.123 = (bf16[3584,512]{1,0:T(8,128)(2,1)S(1)}, bf16[256,3584]{1,0:T(8,128)(2,1)S(1)}, bf16[512,3584]{1,0:T(8,128)(2,1)S(1)}, bf16[3584,256]{1,0:T(8,128)(2,1)S(1)}) custom-call(bf16[3584,128]{1,0:T(8,128)(2,1)} %bitcast.15, bf16[3584,128]{1,0:T(8,128)(2,1)} %bitcast.17, bf16[128,3584]{1,0:T(8,128)(2,1)} %bitcast.19), custom_call_target="tpu_custom_call" | custom-call | tf_op jit(solution)/shard_map/pallas_call | solution.py:22
  11.6 0.0 copy-done
  11.6 0.3 shard_map.125
  12.0 0.0 collective-permute-done.1.refs_1_
  12.0 0.0 collective-permute-done.2.refs_2_
  12.0 0.0 copy-start.1
  12.0 1.3 %shard_map.124 = (bf16[3584,512]{1,0:T(8,128)(2,1)S(1)}, bf16[256,3584]{1,0:T(8,128)(2,1)S(1)}, bf16[512,3584]{1,0:T(8,128)(2,1)S(1)}, bf16[3584,256]{1,0:T(8,128)(2,1)S(1)}) custom-call(bf16[3584,128]{1,0:T(8,128)(2,1)S(1)} %collective-permute-done.refs_0_, ...), custom_call_target="tpu_custom_call", output_to_operand_aliasing={{0}: (3, {}), {1}: (4, {}), {2}: (5, {}), {3}: (6, {})} | custom-call | tf_op jit(solution)/shard_map/pallas_call | solution.py:22
  13.3 0.0 collective-permute-done.3.refs_1_
  13.3 2.1 %collective-permute-done.4.refs_2_ = bf16[8,9600]{1,0:T(8,128)(2,1)S(1)} collective-permute-done((bf16[8,9600]{1,0:T(8,128)(2,1)S(1)}, bf16[8,9600]{1,0:T(8,128)(2,1)S(1)}, u32[]{:S(2)}, u32[]{:S(2)}) %collective-permute-start.4) | collective-permute-done | bytes 153632 | tf_op jit(solution)/shard_map/ppermute | solution.py:44
  15.4 0.0 collective-permute-done.5.refs_3_
  15.4 0.0 copy-done.1
  15.4 2.5 %shard_map.126 = (bf16[8,6272]{1,0:T(8,128)(2,1)S(1)}, bf16[8,6272]{1,0:T(8,128)(2,1)S(1)}, bf16[8,6272]{1,0:T(8,128)(2,1)S(1)}, bf16[8,6272]{1,0:T(8,128)(2,1)S(1)}) custom-call(f32[1,3584]{1,0:T(1,128)S(1)} %copy-done.1, bf16[3584,512]{1,0:T(8,128)(2,1)S(1)} %get-tuple-element.86.cols_ref, bf16[256,3584]{1,0:T(8,128)(2,1)S(1)} %get-tuple-element.87.rows_ref, ...), custom_call_target="tpu_custom_call" | custom-call | tf_op jit(solution)/shard_map/pallas_call | solution.py:22
  17.8 1.3 %collective-permute-start.6 = (bf16[8,6272]{1,0:T(8,128)(2,1)S(1)}, bf16[8,6272]{1,0:T(8,128)(2,1)S(1)}, u32[]{:S(2)}, u32[]{:S(2)}) collective-permute-start(bf16[8,6272]{1,0:T(8,128)(2,1)S(1)} %get-tuple-element.97), channel_id=1, source_target_pairs={{0,2},{1,3},{2,0},{3,1},{4,6},{5,7},{6,4},{7,5},{8,10},{9,11},{10,... | collective-permute-start | bytes 301064 | tf_op jit(solution)/shard_map/ppermute | solution.py:44
  19.1 0.8 %collective-permute-start.7 = (bf16[8,6272]{1,0:T(8,128)(2,1)S(1)}, bf16[8,6272]{1,0:T(8,128)(2,1)S(1)}, u32[]{:S(2)}, u32[]{:S(2)}) collective-permute-start(bf16[8,6272]{1,0:T(8,128)(2,1)S(1)} %get-tuple-element.98), channel_id=1, source_target_pairs={{0,4},{1,5},{2,6},{3,7},{4,0},{5,1},{6,2},{7,3},{8,12},{9,13},{10,... | collective-permute-start | bytes 301064 | tf_op jit(solution)/shard_map/ppermute | solution.py:44
  19.9 1.4 %collective-permute-start.8 = (bf16[8,6272]{1,0:T(8,128)(2,1)S(1)}, bf16[8,6272]{1,0:T(8,128)(2,1)S(1)}, u32[]{:S(2)}, u32[]{:S(2)}) collective-permute-start(bf16[8,6272]{1,0:T(8,128)(2,1)S(1)} %get-tuple-element.99), channel_id=1, source_target_pairs={{0,6},{1,7},{2,4},{3,5},{4,2},{5,3},{6,0},{7,1},{8,14},{9,15},{10,... | collective-permute-start | bytes 301064 | tf_op jit(solution)/shard_map/ppermute | solution.py:44
  21.4 1.5 %collective-permute-done.6.refs_1_ = bf16[8,6272]{1,0:T(8,128)(2,1)S(1)} collective-permute-done((bf16[8,6272]{1,0:T(8,128)(2,1)S(1)}, bf16[8,6272]{1,0:T(8,128)(2,1)S(1)}, u32[]{:S(2)}, u32[]{:S(2)}) %collective-permute-start.6) | collective-permute-done | bytes 100384 | tf_op jit(solution)/shard_map/ppermute | solution.py:44
  22.9 1.6 %collective-permute-done.7.refs_2_ = bf16[8,6272]{1,0:T(8,128)(2,1)S(1)} collective-permute-done((bf16[8,6272]{1,0:T(8,128)(2,1)S(1)}, bf16[8,6272]{1,0:T(8,128)(2,1)S(1)}, u32[]{:S(2)}, u32[]{:S(2)}) %collective-permute-start.7) | collective-permute-done | bytes 100384 | tf_op jit(solution)/shard_map/ppermute | solution.py:44
  24.5 1.1 %collective-permute-done.8.refs_3_ = bf16[8,6272]{1,0:T(8,128)(2,1)S(1)} collective-permute-done((bf16[8,6272]{1,0:T(8,128)(2,1)S(1)}, bf16[8,6272]{1,0:T(8,128)(2,1)S(1)}, u32[]{:S(2)}, u32[]{:S(2)}) %collective-permute-start.8) | collective-permute-done | bytes 100384 | tf_op jit(solution)/shard_map/ppermute | solution.py:44
  25.5 0.4 shard_map.127
  26.0 0.1 collective-permute-start.10
  26.0 3.1 %collective-permute-start.9 = (bf16[24,3584]{1,0:T(8,128)(2,1)S(1)}, bf16[24,3584]{1,0:T(8,128)(2,1)S(1)}, u32[]{:S(2)}, u32[]{:S(2)}) collective-permute-start(bf16[24,3584]{1,0:T(8,128)(2,1)S(1)} %get-tuple-element.106), channel_id=1, source_target_pairs={{0,8},{1,9},{2,10},{3,11},{4,12},{5,13},{6,14},{7,15},{8,0},{9,1},... | collective-permute-start | bytes 516104 | tf_op jit(solution)/shard_map/ppermute | solution.py:55
  29.2 1.4 %collective-permute-start.14 = (bf16[8,3584]{1,0:T(8,128)(2,1)S(1)}, bf16[8,3584]{1,0:T(8,128)(2,1)S(1)}, u32[]{:S(2)}, u32[]{:S(2)}) collective-permute-start(bf16[8,3584]{1,0:T(8,128)(2,1)S(1)} %get-tuple-element.113), channel_id=1, source_target_pairs={{0,2},{1,3},{2,0},{3,1},{4,6},{5,7},{6,4},{7,5},{8,10},{9,11},{10,... | collective-permute-start | bytes 172040 | tf_op jit(solution)/shard_map/ppermute | solution.py:44
  30.6 0.0 collective-permute-done.10.high
  30.6 2.2 %collective-permute-done.9.low = bf16[24,3584]{1,0:T(8,128)(2,1)S(1)} collective-permute-done((bf16[24,3584]{1,0:T(8,128)(2,1)S(1)}, bf16[24,3584]{1,0:T(8,128)(2,1)S(1)}, u32[]{:S(2)}, u32[]{:S(2)}) %collective-permute-start.9) | collective-permute-done | bytes 172064 | tf_op jit(solution)/shard_map/ppermute | solution.py:55
  32.8 0.3 shard_map.128
  33.1 1.5 %collective-permute-start.11 = (bf16[8,6400]{1,0:T(8,128)(2,1)S(1)}, bf16[8,6400]{1,0:T(8,128)(2,1)S(1)}, u32[]{:S(2)}, u32[]{:S(2)}) collective-permute-start(bf16[8,6400]{1,0:T(8,128)(2,1)S(1)} %get-tuple-element.109), channel_id=1, source_target_pairs={{0,2},{1,3},{2,0},{3,1},{4,6},{5,7},{6,4},{7,5},{8,10},{9,11},{10,... | collective-permute-start | bytes 307208 | tf_op jit(solution)/shard_map/ppermute | solution.py:44
  34.6 0.9 %collective-permute-start.12 = (bf16[8,6400]{1,0:T(8,128)(2,1)S(1)}, bf16[8,6400]{1,0:T(8,128)(2,1)S(1)}, u32[]{:S(2)}, u32[]{:S(2)}) collective-permute-start(bf16[8,6400]{1,0:T(8,128)(2,1)S(1)} %get-tuple-element.110), channel_id=1, source_target_pairs={{0,4},{1,5},{2,6},{3,7},{4,0},{5,1},{6,2},{7,3},{8,12},{9,13},{10,... | collective-permute-start | bytes 307208 | tf_op jit(solution)/shard_map/ppermute | solution.py:44
  35.5 1.2 %collective-permute-start.13 = (bf16[8,6400]{1,0:T(8,128)(2,1)S(1)}, bf16[8,6400]{1,0:T(8,128)(2,1)S(1)}, u32[]{:S(2)}, u32[]{:S(2)}) collective-permute-start(bf16[8,6400]{1,0:T(8,128)(2,1)S(1)} %get-tuple-element.111), channel_id=1, source_target_pairs={{0,6},{1,7},{2,4},{3,5},{4,2},{5,3},{6,0},{7,1},{8,14},{9,15},{10,... | collective-permute-start | bytes 307208 | tf_op jit(solution)/shard_map/ppermute | solution.py:44
  36.7 1.2 %collective-permute-start.15 = (bf16[8,3584]{1,0:T(8,128)(2,1)S(1)}, bf16[8,3584]{1,0:T(8,128)(2,1)S(1)}, u32[]{:S(2)}, u32[]{:S(2)}) collective-permute-start(bf16[8,3584]{1,0:T(8,128)(2,1)S(1)} %get-tuple-element.114), channel_id=1, source_target_pairs={{0,4},{1,5},{2,6},{3,7},{4,0},{5,1},{6,2},{7,3},{8,12},{9,13},{10,... | collective-permute-start | bytes 172040 | tf_op jit(solution)/shard_map/ppermute | solution.py:44
  37.9 0.0 collective-permute-done.14.refs_5_
  37.9 1.7 %collective-permute-start.16 = (bf16[8,3584]{1,0:T(8,128)(2,1)S(1)}, bf16[8,3584]{1,0:T(8,128)(2,1)S(1)}, u32[]{:S(2)}, u32[]{:S(2)}) collective-permute-start(bf16[8,3584]{1,0:T(8,128)(2,1)S(1)} %get-tuple-element.115), channel_id=1, source_target_pairs={{0,6},{1,7},{2,4},{3,5},{4,2},{5,3},{6,0},{7,1},{8,14},{9,15},{10,... | collective-permute-start | bytes 172040 | tf_op jit(solution)/shard_map/ppermute | solution.py:44
  39.6 2.5 %collective-permute-done.15.refs_6_ = bf16[8,3584]{1,0:T(8,128)(2,1)S(1)} collective-permute-done((bf16[8,3584]{1,0:T(8,128)(2,1)S(1)}, bf16[8,3584]{1,0:T(8,128)(2,1)S(1)}, u32[]{:S(2)}, u32[]{:S(2)}) %collective-permute-start.15) | collective-permute-done | bytes 57376 | tf_op jit(solution)/shard_map/ppermute | solution.py:44
  42.1 0.9 %collective-permute-done.16.refs_7_ = bf16[8,3584]{1,0:T(8,128)(2,1)S(1)} collective-permute-done((bf16[8,3584]{1,0:T(8,128)(2,1)S(1)}, bf16[8,3584]{1,0:T(8,128)(2,1)S(1)}, u32[]{:S(2)}, u32[]{:S(2)}) %collective-permute-start.16) | collective-permute-done | bytes 57376 | tf_op jit(solution)/shard_map/ppermute | solution.py:44
  43.0 0.0 collective-permute-done.11.refs_1_
  43.0 0.0 collective-permute-done.12.refs_2_
  43.0 0.0 collective-permute-done.13.refs_3_
  43.0 2.3 %shard_map.129 = (bf16[8,6272]{1,0:T(8,128)(2,1)S(1)}, bf16[8,6272]{1,0:T(8,128)(2,1)S(1)}, bf16[8,6272]{1,0:T(8,128)(2,1)S(1)}, bf16[8,6272]{1,0:T(8,128)(2,1)S(1)}) custom-call(f32[1,3584]{1,0:T(1,128)S(1)} %copy-done.1, bf16[3584,512]{1,0:T(8,128)(2,1)S(1)} %get-tuple-element.86.cols_ref, bf16[256,3584]{1,0:T(8,128)(2,1)S(1)} %get-tuple-element.87.rows_ref, ...), custom_call_target="tpu_custom_call" | custom-call | tf_op jit(solution)/shard_map/pallas_call | solution.py:22
  45.3 1.2 %collective-permute-start.17 = (bf16[8,6272]{1,0:T(8,128)(2,1)S(1)}, bf16[8,6272]{1,0:T(8,128)(2,1)S(1)}, u32[]{:S(2)}, u32[]{:S(2)}) collective-permute-start(bf16[8,6272]{1,0:T(8,128)(2,1)S(1)} %get-tuple-element.117), channel_id=1, source_target_pairs={{0,2},{1,3},{2,0},{3,1},{4,6},{5,7},{6,4},{7,5},{8,10},{9,11},{10,... | collective-permute-start | bytes 301064 | tf_op jit(solution)/shard_map/ppermute | solution.py:44
  46.5 1.2 %collective-permute-start.18 = (bf16[8,6272]{1,0:T(8,128)(2,1)S(1)}, bf16[8,6272]{1,0:T(8,128)(2,1)S(1)}, u32[]{:S(2)}, u32[]{:S(2)}) collective-permute-start(bf16[8,6272]{1,0:T(8,128)(2,1)S(1)} %get-tuple-element.118), channel_id=1, source_target_pairs={{0,4},{1,5},{2,6},{3,7},{4,0},{5,1},{6,2},{7,3},{8,12},{9,13},{10,... | collective-permute-start | bytes 301064 | tf_op jit(solution)/shard_map/ppermute | solution.py:44
  47.6 1.2 %collective-permute-start.19 = (bf16[8,6272]{1,0:T(8,128)(2,1)S(1)}, bf16[8,6272]{1,0:T(8,128)(2,1)S(1)}, u32[]{:S(2)}, u32[]{:S(2)}) collective-permute-start(bf16[8,6272]{1,0:T(8,128)(2,1)S(1)} %get-tuple-element.119), channel_id=1, source_target_pairs={{0,6},{1,7},{2,4},{3,5},{4,2},{5,3},{6,0},{7,1},{8,14},{9,15},{10,... | collective-permute-start | bytes 301064 | tf_op jit(solution)/shard_map/ppermute | solution.py:44
  48.9 1.1 %collective-permute-done.17.refs_1_ = bf16[8,6272]{1,0:T(8,128)(2,1)S(1)} collective-permute-done((bf16[8,6272]{1,0:T(8,128)(2,1)S(1)}, bf16[8,6272]{1,0:T(8,128)(2,1)S(1)}, u32[]{:S(2)}, u32[]{:S(2)}) %collective-permute-start.17) | collective-permute-done | bytes 100384 | tf_op jit(solution)/shard_map/ppermute | solution.py:44
  50.0 1.1 %collective-permute-done.18.refs_2_ = bf16[8,6272]{1,0:T(8,128)(2,1)S(1)} collective-permute-done((bf16[8,6272]{1,0:T(8,128)(2,1)S(1)}, bf16[8,6272]{1,0:T(8,128)(2,1)S(1)}, u32[]{:S(2)}, u32[]{:S(2)}) %collective-permute-start.18) | collective-permute-done | bytes 100384 | tf_op jit(solution)/shard_map/ppermute | solution.py:44
  51.1 2.1 %collective-permute-done.19.refs_3_ = bf16[8,6272]{1,0:T(8,128)(2,1)S(1)} collective-permute-done((bf16[8,6272]{1,0:T(8,128)(2,1)S(1)}, bf16[8,6272]{1,0:T(8,128)(2,1)S(1)}, u32[]{:S(2)}, u32[]{:S(2)}) %collective-permute-start.19) | collective-permute-done | bytes 100384 | tf_op jit(solution)/shard_map/ppermute | solution.py:44
  53.2 0.9 %shard_map.130 = (bf16[24,3584]{1,0:T(8,128)(2,1)}, bf16[24,3584]{1,0:T(8,128)(2,1)}) custom-call(bf16[4,24,32]{2,1,0:T(8,128)(2,1)S(1)} %get-tuple-element.85.tables, bf16[8,6272]{1,0:T(8,128)(2,1)S(1)} %get-tuple-element.116.refs_0_, bf16[8,6272]{1,0:T(8,128)(2,1)S(1)} %collective-permute-done.17.refs_1_, ...), custom_call_target="tpu_custom_call" | custom-call | tf_op jit(solution)/shard_map/pallas_call | solution.py:22
Async XLA Ops:
  0.6 11.0 %copy-start = (bf16[1,2,24,3584]{3,2,1,0:T(8,128)(2,1)S(1)}, bf16[1,2,24,3584]{3,2,1,0:T(8,128)(2,1)}, u32[]{:S(2)}) copy-start(bf16[1,2,24,3584]{3,2,1,0:T(8,128)(2,1)} %param.13) | copy-start | bytes 1032196
  2.4 5.2 %collective-permute-start = (bf16[3584,128]{1,0:T(8,128)(2,1)}, bf16[3584,128]{1,0:T(8,128)(2,1)S(1)}, u32[]{:S(2)}, u32[]{:S(2)}) collective-permute-start(bf16[3584,128]{1,0:T(8,128)(2,1)} %bitcast.14), channel_id=1, source_target_pairs={{0,1},{1,0},{2,3},{3,2},{4,5},{5,4},{6,7},{7,6},{8,9},{9,8},{10,11... | collective-permute-start | bytes 2752520 | tf_op jit(solution)/shard_map/ppermute | solution.py:37
  3.0 9.0 %collective-permute-start.1 = (bf16[3584,128]{1,0:T(8,128)(2,1)}, bf16[3584,128]{1,0:T(8,128)(2,1)S(1)}, u32[]{:S(2)}, u32[]{:S(2)}) collective-permute-start(bf16[3584,128]{1,0:T(8,128)(2,1)} %bitcast.16), channel_id=1, source_target_pairs={{0,1},{1,0},{2,3},{3,2},{4,5},{5,4},{6,7},{7,6},{8,9},{9,8},{10,11... | collective-permute-start | bytes 2752520 | tf_op jit(solution)/shard_map/ppermute | solution.py:37
  3.0 8.9 %collective-permute-start.2 = (bf16[128,3584]{1,0:T(8,128)(2,1)}, bf16[128,3584]{1,0:T(8,128)(2,1)S(1)}, u32[]{:S(2)}, u32[]{:S(2)}) collective-permute-start(bf16[128,3584]{1,0:T(8,128)(2,1)} %bitcast.18), channel_id=1, source_target_pairs={{0,1},{1,0},{2,3},{3,2},{4,5},{5,4},{6,7},{7,6},{8,9},{9,8},{10,11... | collective-permute-start | bytes 2752520 | tf_op jit(solution)/shard_map/ppermute | solution.py:37
  3.5 9.8 %collective-permute-start.3 = (bf16[8,9600]{1,0:T(8,128)(2,1)S(1)}, bf16[8,9600]{1,0:T(8,128)(2,1)S(1)}, u32[]{:S(2)}, u32[]{:S(2)}) collective-permute-start(bf16[8,9600]{1,0:T(8,128)(2,1)S(1)} %get-tuple-element.93), channel_id=1, source_target_pairs={{0,2},{1,3},{2,0},{3,1},{4,6},{5,7},{6,4},{7,5},{8,10},{9,11},{10,... | collective-permute-start | bytes 460808 | tf_op jit(solution)/shard_map/ppermute | solution.py:44
  6.0 9.3 %collective-permute-start.4 = (bf16[8,9600]{1,0:T(8,128)(2,1)S(1)}, bf16[8,9600]{1,0:T(8,128)(2,1)S(1)}, u32[]{:S(2)}, u32[]{:S(2)}) collective-permute-start(bf16[8,9600]{1,0:T(8,128)(2,1)S(1)} %get-tuple-element.94), channel_id=1, source_target_pairs={{0,4},{1,5},{2,6},{3,7},{4,0},{5,1},{6,2},{7,3},{8,12},{9,13},{10,... | collective-permute-start | bytes 460808 | tf_op jit(solution)/shard_map/ppermute | solution.py:44
  7.6 7.8 %collective-permute-start.5 = (bf16[8,9600]{1,0:T(8,128)(2,1)S(1)}, bf16[8,9600]{1,0:T(8,128)(2,1)S(1)}, u32[]{:S(2)}, u32[]{:S(2)}) collective-permute-start(bf16[8,9600]{1,0:T(8,128)(2,1)S(1)} %get-tuple-element.95), channel_id=1, source_target_pairs={{0,6},{1,7},{2,4},{3,5},{4,2},{5,3},{6,0},{7,1},{8,14},{9,15},{10,... | collective-permute-start | bytes 460808 | tf_op jit(solution)/shard_map/ppermute | solution.py:44
  12.0 3.4 %copy-start.1 = (f32[1,3584]{1,0:T(1,128)S(1)}, f32[1,3584]{1,0:T(1,128)}, u32[]{:S(2)}) copy-start(f32[1,3584]{1,0:T(1,128)} %gain_ref.3) | copy-start | bytes 43012
  17.8 5.0 %collective-permute-start.6 = (bf16[8,6272]{1,0:T(8,128)(2,1)S(1)}, bf16[8,6272]{1,0:T(8,128)(2,1)S(1)}, u32[]{:S(2)}, u32[]{:S(2)}) collective-permute-start(bf16[8,6272]{1,0:T(8,128)(2,1)S(1)} %get-tuple-element.97), channel_id=1, source_target_pairs={{0,2},{1,3},{2,0},{3,1},{4,6},{5,7},{6,4},{7,5},{8,10},{9,11},{10,... | collective-permute-start | bytes 301064 | tf_op jit(solution)/shard_map/ppermute | solution.py:44
  19.1 5.4 %collective-permute-start.7 = (bf16[8,6272]{1,0:T(8,128)(2,1)S(1)}, bf16[8,6272]{1,0:T(8,128)(2,1)S(1)}, u32[]{:S(2)}, u32[]{:S(2)}) collective-permute-start(bf16[8,6272]{1,0:T(8,128)(2,1)S(1)} %get-tuple-element.98), channel_id=1, source_target_pairs={{0,4},{1,5},{2,6},{3,7},{4,0},{5,1},{6,2},{7,3},{8,12},{9,13},{10,... | collective-permute-start | bytes 301064 | tf_op jit(solution)/shard_map/ppermute | solution.py:44
  19.9 5.6 %collective-permute-start.8 = (bf16[8,6272]{1,0:T(8,128)(2,1)S(1)}, bf16[8,6272]{1,0:T(8,128)(2,1)S(1)}, u32[]{:S(2)}, u32[]{:S(2)}) collective-permute-start(bf16[8,6272]{1,0:T(8,128)(2,1)S(1)} %get-tuple-element.99), channel_id=1, source_target_pairs={{0,6},{1,7},{2,4},{3,5},{4,2},{5,3},{6,0},{7,1},{8,14},{9,15},{10,... | collective-permute-start | bytes 301064 | tf_op jit(solution)/shard_map/ppermute | solution.py:44
  26.0 4.6 %collective-permute-start.10 = (bf16[24,3584]{1,0:T(8,128)(2,1)S(1)}, bf16[24,3584]{1,0:T(8,128)(2,1)S(1)}, u32[]{:S(2)}, u32[]{:S(2)}) collective-permute-start(bf16[24,3584]{1,0:T(8,128)(2,1)S(1)} %get-tuple-element.107), channel_id=1, source_target_pairs={{0,1},{1,0},{2,3},{3,2},{4,5},{5,4},{6,7},{7,6},{8,16},{9,17},{10,... | collective-permute-start | bytes 516104 | tf_op jit(solution)/shard_map/ppermute | solution.py:55
  26.0 6.8 %collective-permute-start.9 = (bf16[24,3584]{1,0:T(8,128)(2,1)S(1)}, bf16[24,3584]{1,0:T(8,128)(2,1)S(1)}, u32[]{:S(2)}, u32[]{:S(2)}) collective-permute-start(bf16[24,3584]{1,0:T(8,128)(2,1)S(1)} %get-tuple-element.106), channel_id=1, source_target_pairs={{0,8},{1,9},{2,10},{3,11},{4,12},{5,13},{6,14},{7,15},{8,0},{9,1},... | collective-permute-start | bytes 516104 | tf_op jit(solution)/shard_map/ppermute | solution.py:55
  29.2 8.7 %collective-permute-start.14 = (bf16[8,3584]{1,0:T(8,128)(2,1)S(1)}, bf16[8,3584]{1,0:T(8,128)(2,1)S(1)}, u32[]{:S(2)}, u32[]{:S(2)}) collective-permute-start(bf16[8,3584]{1,0:T(8,128)(2,1)S(1)} %get-tuple-element.113), channel_id=1, source_target_pairs={{0,2},{1,3},{2,0},{3,1},{4,6},{5,7},{6,4},{7,5},{8,10},{9,11},{10,... | collective-permute-start | bytes 172040 | tf_op jit(solution)/shard_map/ppermute | solution.py:44
  33.1 9.8 %collective-permute-start.11 = (bf16[8,6400]{1,0:T(8,128)(2,1)S(1)}, bf16[8,6400]{1,0:T(8,128)(2,1)S(1)}, u32[]{:S(2)}, u32[]{:S(2)}) collective-permute-start(bf16[8,6400]{1,0:T(8,128)(2,1)S(1)} %get-tuple-element.109), channel_id=1, source_target_pairs={{0,2},{1,3},{2,0},{3,1},{4,6},{5,7},{6,4},{7,5},{8,10},{9,11},{10,... | collective-permute-start | bytes 307208 | tf_op jit(solution)/shard_map/ppermute | solution.py:44
  34.6 8.3 %collective-permute-start.12 = (bf16[8,6400]{1,0:T(8,128)(2,1)S(1)}, bf16[8,6400]{1,0:T(8,128)(2,1)S(1)}, u32[]{:S(2)}, u32[]{:S(2)}) collective-permute-start(bf16[8,6400]{1,0:T(8,128)(2,1)S(1)} %get-tuple-element.110), channel_id=1, source_target_pairs={{0,4},{1,5},{2,6},{3,7},{4,0},{5,1},{6,2},{7,3},{8,12},{9,13},{10,... | collective-permute-start | bytes 307208 | tf_op jit(solution)/shard_map/ppermute | solution.py:44
  35.5 7.5 %collective-permute-start.13 = (bf16[8,6400]{1,0:T(8,128)(2,1)S(1)}, bf16[8,6400]{1,0:T(8,128)(2,1)S(1)}, u32[]{:S(2)}, u32[]{:S(2)}) collective-permute-start(bf16[8,6400]{1,0:T(8,128)(2,1)S(1)} %get-tuple-element.111), channel_id=1, source_target_pairs={{0,6},{1,7},{2,4},{3,5},{4,2},{5,3},{6,0},{7,1},{8,14},{9,15},{10,... | collective-permute-start | bytes 307208 | tf_op jit(solution)/shard_map/ppermute | solution.py:44
  36.7 5.4 %collective-permute-start.15 = (bf16[8,3584]{1,0:T(8,128)(2,1)S(1)}, bf16[8,3584]{1,0:T(8,128)(2,1)S(1)}, u32[]{:S(2)}, u32[]{:S(2)}) collective-permute-start(bf16[8,3584]{1,0:T(8,128)(2,1)S(1)} %get-tuple-element.114), channel_id=1, source_target_pairs={{0,4},{1,5},{2,6},{3,7},{4,0},{5,1},{6,2},{7,3},{8,12},{9,13},{10,... | collective-permute-start | bytes 172040 | tf_op jit(solution)/shard_map/ppermute | solution.py:44
  37.9 5.1 %collective-permute-start.16 = (bf16[8,3584]{1,0:T(8,128)(2,1)S(1)}, bf16[8,3584]{1,0:T(8,128)(2,1)S(1)}, u32[]{:S(2)}, u32[]{:S(2)}) collective-permute-start(bf16[8,3584]{1,0:T(8,128)(2,1)S(1)} %get-tuple-element.115), channel_id=1, source_target_pairs={{0,6},{1,7},{2,4},{3,5},{4,2},{5,3},{6,0},{7,1},{8,14},{9,15},{10,... | collective-permute-start | bytes 172040 | tf_op jit(solution)/shard_map/ppermute | solution.py:44
  45.3 4.7 %collective-permute-start.17 = (bf16[8,6272]{1,0:T(8,128)(2,1)S(1)}, bf16[8,6272]{1,0:T(8,128)(2,1)S(1)}, u32[]{:S(2)}, u32[]{:S(2)}) collective-permute-start(bf16[8,6272]{1,0:T(8,128)(2,1)S(1)} %get-tuple-element.117), channel_id=1, source_target_pairs={{0,2},{1,3},{2,0},{3,1},{4,6},{5,7},{6,4},{7,5},{8,10},{9,11},{10,... | collective-permute-start | bytes 301064 | tf_op jit(solution)/shard_map/ppermute | solution.py:44
  46.5 4.6 %collective-permute-start.18 = (bf16[8,6272]{1,0:T(8,128)(2,1)S(1)}, bf16[8,6272]{1,0:T(8,128)(2,1)S(1)}, u32[]{:S(2)}, u32[]{:S(2)}) collective-permute-start(bf16[8,6272]{1,0:T(8,128)(2,1)S(1)} %get-tuple-element.118), channel_id=1, source_target_pairs={{0,4},{1,5},{2,6},{3,7},{4,0},{5,1},{6,2},{7,3},{8,12},{9,13},{10,... | collective-permute-start | bytes 301064 | tf_op jit(solution)/shard_map/ppermute | solution.py:44
  47.6 5.5 %collective-permute-start.19 = (bf16[8,6272]{1,0:T(8,128)(2,1)S(1)}, bf16[8,6272]{1,0:T(8,128)(2,1)S(1)}, u32[]{:S(2)}, u32[]{:S(2)}) collective-permute-start(bf16[8,6272]{1,0:T(8,128)(2,1)S(1)} %get-tuple-element.119), channel_id=1, source_target_pairs={{0,6},{1,7},{2,4},{3,5},{4,2},{5,3},{6,0},{7,1},{8,14},{9,15},{10,... | collective-permute-start | bytes 301064 | tf_op jit(solution)/shard_map/ppermute | solution.py:44
where the time goes:
time: 54.3 us; the launch traced here: 54.1 us
  starting transfers between devices  24.9 us (46%)
  waiting for transfers between devices  16.2 us (30%)
  Pallas kernels  12.3 us (23%)
  between operations  0.77 us (1%)
    ppermute x15, starting transfers between devices, exchange(): moved.append(lax.ppermute(pieces[m], 'expert', pairs))  20.6 us
    ppermute x15, waiting for transfers between devices, exchange(): moved.append(lax.ppermute(pieces[m], 'expert', pairs))  13.9 us
    pallas_call x9, Pallas kernels, call(): pl.pallas_call(body, out_shape=outs, compiler_params=pltpu.CompilerParams...  12.3 us
    ppermute x2, starting transfers between devices, swap_ranks(): return lax.ppermute(array, ('pipe', 'expert'), list(enumerate(target)))  3.21 us
    ppermute x2, waiting for transfers between devices, swap_ranks(): return lax.ppermute(array, ('pipe', 'expert'), list(enumerate(target)))  2.21 us
  transfers between devices with their start and end apart: 20, of which 10 were waited for; matrix products, arithmetic and copies ran while one was open for 0% of the time, Pallas kernels for 8%

commit v1 on v0

--- a/solution.py
+++ b/solution.py
@@ -136,11 +136,13 @@
 
 def first_spread_body(steps, tokens, *refs):
     small, (state, grad, saved), refs = refs[:4], refs[4:7], refs[7:]
-    lines, outs, scratch, sems = refs[0], refs[1 : 1 + EXPERTS], refs[1 + EXPERTS : -1], refs[-1]
+    lines, held, tables, gates, out, scratch, sems = (
+        refs[0], refs[1:4], refs[4], refs[5], refs[6], refs[7:-1], refs[-1]
+    )
     sources = [*small, state, grad, saved.at[pl.ds(0, tokens), :]]
     copies = [
         pltpu.make_async_copy(src, dst, sems.at[i])
-        for i, (src, dst) in enumerate(zip(sources, scratch))
+        for i, (src, dst) in enumerate(zip(sources, [*scratch, *held]))
     ]
     for copy in copies:
         copy.start()
@@ -149,31 +151,49 @@
         copies[i].wait()
         lines[i * steps : (i + 1) * steps, :tokens] = scratch[i][...].astype(F32)
     routes = jnp.concatenate([scratch[0][0:1], scratch[1][0:1]], axis=0)
-    fwd_hits, bwd_hits = slot_hits(routes)
-    put_pieces(outs, 0, slot_gates(fwd_hits, bwd_hits, scratch[2][0:1], scratch[3][0:1]))
-    fwd_table, bwd_table = as_table(fwd_hits).astype(BF16), as_table(bwd_hits).astype(BF16)
+    hits = slot_hits(routes)
+    value = slot_gates(*hits, scratch[2][0:1], scratch[3][0:1])
+    gates[...] = value.astype(BF16)
+    near = (EXPERTS - 1) * SLOT
+    put_pieces([out], 0, value[near:])
+    made = [as_table(h) for h in hits]
+    for i, table in enumerate(made):
+        tables[i] = table.astype(BF16)
+    far = [table[near:].astype(BF16) for table in made]
     parts = []
-    for i, table in enumerate((fwd_table, bwd_table, bwd_table)):
+    for i, table in enumerate((far[0], far[1], far[1])):
         copies[4 + i].wait()
-        parts.append(placed(table, scratch[4 + i][...]))
-    put_folded(outs, LANES, parts)
+        parts.append(placed(table, held[i][...]))
+    put_folded([out], LANES, parts)
+
+
+def other_spread_body(tables, gates, state, grad, saved, *outs):
+    near = (EXPERTS - 1) * SLOT
+    put_pieces(outs, 0, gates[:near, :].astype(F32))
+    pairs = ((tables[0], state), (tables[1], grad), (tables[1], saved))
+    put_folded(outs, LANES, [placed(table[:near], rows[...]) for table, rows in pairs])
 
 
 def first_spread(small, state, grad, saved):
     steps, tokens = small[0].shape
     width = state.shape[1]
+    slots = EXPERTS * SLOT
+    piece = jax.ShapeDtypeStruct((SLOT, LANES + folded(3 * width)[0]), BF16)
     outs = [jax.ShapeDtypeStruct((-(-4 * steps // 8) * 8, LANES), F32)]
-    outs += [jax.ShapeDtypeStruct((SLOT, LANES + folded(3 * width)[0]), BF16)] * EXPERTS
+    outs += [jax.ShapeDtypeStruct((tokens, width), BF16)] * 3
+    outs += [jax.ShapeDtypeStruct((2, slots, tokens), BF16)]
+    outs += [jax.ShapeDtypeStruct((slots, LANES), BF16), piece]
     args = [*small, state, grad, saved]
-    return call(
+    lines, *held, tables, gates, far = call(
         functools.partial(first_spread_body, steps, tokens),
         outs,
         [pltpu.with_memory_space_constraint(a, pltpu.HBM) for a in args],
         in_specs=[pl.BlockSpec(memory_space=pltpu.HBM)] * len(args),
         scratch_shapes=[pltpu.VMEM((steps, tokens), a.dtype) for a in small]
-        + [pltpu.VMEM((tokens, width), BF16)] * 3
         + [pltpu.SemaphoreType.DMA((len(args),))],
     )
+    near = call(other_spread_body, [piece] * (EXPERTS - 1), [tables, gates, *held])
+    return lines, *near, far
 
 
 def prepare_body(steps, tokens, *refs):
@@ -372,7 +392,7 @@
     saved = saved_input[0].reshape(steps * tokens, width)
     small = [a.reshape(steps, tokens) for a in (fwd_route, bwd_route, fwd_gate, bwd_gate)]
     lines, *made = first_spread(small, fwd_state[0], bwd_state[0], saved)
-    made, own = lax.optimization_barrier((made, (w_gate[0], w_up[0], w_down[0])))
+    lines, own = lax.optimization_barrier((lines, (w_gate[0], w_up[0], w_down[0])))
     pieces = exchange(made)
     weights = pack(own)
     pair = folded(2 * width)[0]

time: 54.3 us -> 54.6 us (level)
    pallas_call x9 -> x10, Pallas kernels: 12.3 us -> 12.5 us  [call(): pl.pallas_call(body, out_shape=outs, compiler_params=pltpu.CompilerParams...]
  transfers between devices with their start and end apart: 20 -> 20, of which waited for: 10 -> 9; matrix products, arithmetic and copies ran while one was open for 0% -> 0% of each run, Pallas kernels for 8% -> 9%
where the time goes in v1:
time: 54.6 us; the launch traced here: 54.4 us
  starting transfers between devices  24.4 us (45%)
  waiting for transfers between devices  16.7 us (31%)
  Pallas kernels  12.5 us (23%)
  between operations  0.78 us (1%)
    ppermute x15, starting transfers between devices, exchange(): moved.append(lax.ppermute(pieces[m], 'expert', pairs))  20.1 us
    ppermute x15, waiting for transfers between devices, exchange(): moved.append(lax.ppermute(pieces[m], 'expert', pairs))  14.5 us
    pallas_call x10, Pallas kernels, call(): pl.pallas_call(body, out_shape=outs, compiler_params=pltpu.CompilerParams...  12.5 us
    ppermute x2, starting transfers between devices, swap_ranks(): return lax.ppermute(array, ('pipe', 'expert'), list(enumerate(target)))  3.15 us
    ppermute x2, waiting for transfers between devices, swap_ranks(): return lax.ppermute(array, ('pipe', 'expert'), list(enumerate(target)))  2.26 us
  transfers between devices with their start and end apart: 20, of which 9 were waited for; matrix products, arithmetic and copies ran while one was open for 0% of the time, Pallas kernels for 9%

profile of v1, /device:TPU:0, one launch (start us, length us, event | category | flops | bytes accessed | tf_op | source)
XLA Modules:
  0.0 54.4 jit_solution(6487367534170469357)
XLA Ops:
  0.6 0.0 copy-start
  0.6 1.6 %shard_map.122 = (f32[8,128]{1,0:T(8,128)S(1)}, bf16[24,3584]{1,0:T(8,128)(2,1)S(1)}, bf16[24,3584]{1,0:T(8,128)(2,1)S(1)}, bf16[24,3584]{1,0:T(8,128)(2,1)S(1)}...) custom-call(s32[2,24]{1,0:T(2,128)} %bitcast.22, s32[2,24]{1,0:T(2,128)} %bitcast.23, ...), custom_call_target="tpu_custom_call" | custom-call | tf_op jit(solution)/shard_map/pallas_call | solution.py:22
  2.2 0.6 %collective-permute-start = (bf16[3584,128]{1,0:T(8,128)(2,1)}, bf16[3584,128]{1,0:T(8,128)(2,1)S(1)}, u32[]{:S(2)}, u32[]{:S(2)}) collective-permute-start(bf16[3584,128]{1,0:T(8,128)(2,1)} %bitcast.14), channel_id=1, source_target_pairs={{0,1},{1,0},{2,3},{3,2},{4,5},{5,4},{6,7},{7,6},{8,9},{9,8},{10,11... | collective-permute-start | bytes 2752520 | tf_op jit(solution)/shard_map/ppermute | solution.py:37
  2.8 0.1 collective-permute-start.1
  2.9 0.4 collective-permute-start.2
  3.3 0.4 shard_map.126
  3.7 2.6 %collective-permute-start.3 = (bf16[8,9600]{1,0:T(8,128)(2,1)S(1)}, bf16[8,9600]{1,0:T(8,128)(2,1)S(1)}, u32[]{:S(2)}, u32[]{:S(2)}) collective-permute-start(bf16[8,9600]{1,0:T(8,128)(2,1)S(1)} %get-tuple-element.97), channel_id=1, source_target_pairs={{0,2},{1,3},{2,0},{3,1},{4,6},{5,7},{6,4},{7,5},{8,10},{9,11},{10,... | collective-permute-start | bytes 460808 | tf_op jit(solution)/shard_map/ppermute | solution.py:44
  6.3 1.5 %collective-permute-start.4 = (bf16[8,9600]{1,0:T(8,128)(2,1)S(1)}, bf16[8,9600]{1,0:T(8,128)(2,1)S(1)}, u32[]{:S(2)}, u32[]{:S(2)}) collective-permute-start(bf16[8,9600]{1,0:T(8,128)(2,1)S(1)} %get-tuple-element.98), channel_id=1, source_target_pairs={{0,4},{1,5},{2,6},{3,7},{4,0},{5,1},{6,2},{7,3},{8,12},{9,13},{10,... | collective-permute-start | bytes 460808 | tf_op jit(solution)/shard_map/ppermute | solution.py:44
  7.8 0.0 collective-permute-done.refs_0_
  7.8 1.1 %collective-permute-start.5 = (bf16[8,9600]{1,0:T(8,128)(2,1)S(1)}, bf16[8,9600]{1,0:T(8,128)(2,1)S(1)}, u32[]{:S(2)}, u32[]{:S(2)}) collective-permute-start(bf16[8,9600]{1,0:T(8,128)(2,1)S(1)} %get-tuple-element.99), channel_id=1, source_target_pairs={{0,6},{1,7},{2,4},{3,5},{4,2},{5,3},{6,0},{7,1},{8,14},{9,15},{10,... | collective-permute-start | bytes 460808 | tf_op jit(solution)/shard_map/ppermute | solution.py:44
  8.9 2.5 %shard_map.123 = (bf16[3584,512]{1,0:T(8,128)(2,1)S(1)}, bf16[256,3584]{1,0:T(8,128)(2,1)S(1)}, bf16[512,3584]{1,0:T(8,128)(2,1)S(1)}, bf16[3584,256]{1,0:T(8,128)(2,1)S(1)}) custom-call(bf16[3584,128]{1,0:T(8,128)(2,1)} %bitcast.15, bf16[3584,128]{1,0:T(8,128)(2,1)} %bitcast.17, bf16[128,3584]{1,0:T(8,128)(2,1)} %bitcast.19), custom_call_target="tpu_custom_call" | custom-call | tf_op jit(solution)/shard_map/pallas_call | solution.py:22
  11.4 0.0 copy-done
  11.4 0.3 shard_map.125
  11.8 0.0 collective-permute-done.1.refs_1_
  11.8 0.0 collective-permute-done.2.refs_2_
  11.8 0.0 copy-start.1
  11.8 1.3 %shard_map.124 = (bf16[3584,512]{1,0:T(8,128)(2,1)S(1)}, bf16[256,3584]{1,0:T(8,128)(2,1)S(1)}, bf16[512,3584]{1,0:T(8,128)(2,1)S(1)}, bf16[3584,256]{1,0:T(8,128)(2,1)S(1)}) custom-call(bf16[3584,128]{1,0:T(8,128)(2,1)S(1)} %collective-permute-done.refs_0_, ...), custom_call_target="tpu_custom_call", output_to_operand_aliasing={{0}: (3, {}), {1}: (4, {}), {2}: (5, {}), {3}: (6, {})} | custom-call | tf_op jit(solution)/shard_map/pallas_call | solution.py:22
  13.1 0.0 collective-permute-done.3.refs_1_
  13.1 2.6 %collective-permute-done.4.refs_2_ = bf16[8,9600]{1,0:T(8,128)(2,1)S(1)} collective-permute-done((bf16[8,9600]{1,0:T(8,128)(2,1)S(1)}, bf16[8,9600]{1,0:T(8,128)(2,1)S(1)}, u32[]{:S(2)}, u32[]{:S(2)}) %collective-permute-start.4) | collective-permute-done | bytes 153632 | tf_op jit(solution)/shard_map/ppermute | solution.py:44
  15.7 0.0 collective-permute-done.5.refs_3_
  15.7 0.0 copy-done.1
  15.7 2.4 %shard_map.127 = (bf16[8,6272]{1,0:T(8,128)(2,1)S(1)}, bf16[8,6272]{1,0:T(8,128)(2,1)S(1)}, bf16[8,6272]{1,0:T(8,128)(2,1)S(1)}, bf16[8,6272]{1,0:T(8,128)(2,1)S(1)}) custom-call(f32[1,3584]{1,0:T(1,128)S(1)} %copy-done.1, bf16[3584,512]{1,0:T(8,128)(2,1)S(1)} %get-tuple-element.85.cols_ref, bf16[256,3584]{1,0:T(8,128)(2,1)S(1)} %get-tuple-element.86.rows_ref, ...), custom_call_target="tpu_custom_call" | custom-call | tf_op jit(solution)/shard_map/pallas_call | solution.py:22
  18.1 1.3 %collective-permute-start.6 = (bf16[8,6272]{1,0:T(8,128)(2,1)S(1)}, bf16[8,6272]{1,0:T(8,128)(2,1)S(1)}, u32[]{:S(2)}, u32[]{:S(2)}) collective-permute-start(bf16[8,6272]{1,0:T(8,128)(2,1)S(1)} %get-tuple-element.101), channel_id=1, source_target_pairs={{0,2},{1,3},{2,0},{3,1},{4,6},{5,7},{6,4},{7,5},{8,10},{9,11},{10,... | collective-permute-start | bytes 301064 | tf_op jit(solution)/shard_map/ppermute | solution.py:44
  19.4 0.8 %collective-permute-start.7 = (bf16[8,6272]{1,0:T(8,128)(2,1)S(1)}, bf16[8,6272]{1,0:T(8,128)(2,1)S(1)}, u32[]{:S(2)}, u32[]{:S(2)}) collective-permute-start(bf16[8,6272]{1,0:T(8,128)(2,1)S(1)} %get-tuple-element.102), channel_id=1, source_target_pairs={{0,4},{1,5},{2,6},{3,7},{4,0},{5,1},{6,2},{7,3},{8,12},{9,13},{10,... | collective-permute-start | bytes 301064 | tf_op jit(solution)/shard_map/ppermute | solution.py:44
  20.2 1.5 %collective-permute-start.8 = (bf16[8,6272]{1,0:T(8,128)(2,1)S(1)}, bf16[8,6272]{1,0:T(8,128)(2,1)S(1)}, u32[]{:S(2)}, u32[]{:S(2)}) collective-permute-start(bf16[8,6272]{1,0:T(8,128)(2,1)S(1)} %get-tuple-element.103), channel_id=1, source_target_pairs={{0,6},{1,7},{2,4},{3,5},{4,2},{5,3},{6,0},{7,1},{8,14},{9,15},{10,... | collective-permute-start | bytes 301064 | tf_op jit(solution)/shard_map/ppermute | solution.py:44
  21.7 1.5 %collective-permute-done.6.refs_1_ = bf16[8,6272]{1,0:T(8,128)(2,1)S(1)} collective-permute-done((bf16[8,6272]{1,0:T(8,128)(2,1)S(1)}, bf16[8,6272]{1,0:T(8,128)(2,1)S(1)}, u32[]{:S(2)}, u32[]{:S(2)}) %collective-permute-start.6) | collective-permute-done | bytes 100384 | tf_op jit(solution)/shard_map/ppermute | solution.py:44
  23.2 2.7 %collective-permute-done.7.refs_2_ = bf16[8,6272]{1,0:T(8,128)(2,1)S(1)} collective-permute-done((bf16[8,6272]{1,0:T(8,128)(2,1)S(1)}, bf16[8,6272]{1,0:T(8,128)(2,1)S(1)}, u32[]{:S(2)}, u32[]{:S(2)}) %collective-permute-start.7) | collective-permute-done | bytes 100384 | tf_op jit(solution)/shard_map/ppermute | solution.py:44
  25.9 0.0 collective-permute-done.8.refs_3_
  25.9 0.4 shard_map.128
  26.3 0.1 collective-permute-start.10
  26.4 3.1 %collective-permute-start.9 = (bf16[24,3584]{1,0:T(8,128)(2,1)S(1)}, bf16[24,3584]{1,0:T(8,128)(2,1)S(1)}, u32[]{:S(2)}, u32[]{:S(2)}) collective-permute-start(bf16[24,3584]{1,0:T(8,128)(2,1)S(1)} %get-tuple-element.110), channel_id=1, source_target_pairs={{0,8},{1,9},{2,10},{3,11},{4,12},{5,13},{6,14},{7,15},{8,0},{9,1},... | collective-permute-start | bytes 516104 | tf_op jit(solution)/shard_map/ppermute | solution.py:55
  29.4 1.4 %collective-permute-start.14 = (bf16[8,3584]{1,0:T(8,128)(2,1)S(1)}, bf16[8,3584]{1,0:T(8,128)(2,1)S(1)}, u32[]{:S(2)}, u32[]{:S(2)}) collective-permute-start(bf16[8,3584]{1,0:T(8,128)(2,1)S(1)} %get-tuple-element.117), channel_id=1, source_target_pairs={{0,2},{1,3},{2,0},{3,1},{4,6},{5,7},{6,4},{7,5},{8,10},{9,11},{10,... | collective-permute-start | bytes 172040 | tf_op jit(solution)/shard_map/ppermute | solution.py:44
  30.9 0.0 collective-permute-done.10.high
  30.9 2.3 %collective-permute-done.9.low = bf16[24,3584]{1,0:T(8,128)(2,1)S(1)} collective-permute-done((bf16[24,3584]{1,0:T(8,128)(2,1)S(1)}, bf16[24,3584]{1,0:T(8,128)(2,1)S(1)}, u32[]{:S(2)}, u32[]{:S(2)}) %collective-permute-start.9) | collective-permute-done | bytes 172064 | tf_op jit(solution)/shard_map/ppermute | solution.py:55
  33.1 0.3 shard_map.129
  33.5 1.5 %collective-permute-start.11 = (bf16[8,6400]{1,0:T(8,128)(2,1)S(1)}, bf16[8,6400]{1,0:T(8,128)(2,1)S(1)}, u32[]{:S(2)}, u32[]{:S(2)}) collective-permute-start(bf16[8,6400]{1,0:T(8,128)(2,1)S(1)} %get-tuple-element.113), channel_id=1, source_target_pairs={{0,2},{1,3},{2,0},{3,1},{4,6},{5,7},{6,4},{7,5},{8,10},{9,11},{10,... | collective-permute-start | bytes 307208 | tf_op jit(solution)/shard_map/ppermute | solution.py:44
  34.9 0.9 %collective-permute-start.12 = (bf16[8,6400]{1,0:T(8,128)(2,1)S(1)}, bf16[8,6400]{1,0:T(8,128)(2,1)S(1)}, u32[]{:S(2)}, u32[]{:S(2)}) collective-permute-start(bf16[8,6400]{1,0:T(8,128)(2,1)S(1)} %get-tuple-element.114), channel_id=1, source_target_pairs={{0,4},{1,5},{2,6},{3,7},{4,0},{5,1},{6,2},{7,3},{8,12},{9,13},{10,... | collective-permute-start | bytes 307208 | tf_op jit(solution)/shard_map/ppermute | solution.py:44
  35.8 1.2 %collective-permute-start.13 = (bf16[8,6400]{1,0:T(8,128)(2,1)S(1)}, bf16[8,6400]{1,0:T(8,128)(2,1)S(1)}, u32[]{:S(2)}, u32[]{:S(2)}) collective-permute-start(bf16[8,6400]{1,0:T(8,128)(2,1)S(1)} %get-tuple-element.115), channel_id=1, source_target_pairs={{0,6},{1,7},{2,4},{3,5},{4,2},{5,3},{6,0},{7,1},{8,14},{9,15},{10,... | collective-permute-start | bytes 307208 | tf_op jit(solution)/shard_map/ppermute | solution.py:44
  37.0 1.1 %collective-permute-start.15 = (bf16[8,3584]{1,0:T(8,128)(2,1)S(1)}, bf16[8,3584]{1,0:T(8,128)(2,1)S(1)}, u32[]{:S(2)}, u32[]{:S(2)}) collective-permute-start(bf16[8,3584]{1,0:T(8,128)(2,1)S(1)} %get-tuple-element.118), channel_id=1, source_target_pairs={{0,4},{1,5},{2,6},{3,7},{4,0},{5,1},{6,2},{7,3},{8,12},{9,13},{10,... | collective-permute-start | bytes 172040 | tf_op jit(solution)/shard_map/ppermute | solution.py:44
  38.2 0.0 collective-permute-done.14.refs_5_
  38.2 1.7 %collective-permute-start.16 = (bf16[8,3584]{1,0:T(8,128)(2,1)S(1)}, bf16[8,3584]{1,0:T(8,128)(2,1)S(1)}, u32[]{:S(2)}, u32[]{:S(2)}) collective-permute-start(bf16[8,3584]{1,0:T(8,128)(2,1)S(1)} %get-tuple-element.119), channel_id=1, source_target_pairs={{0,6},{1,7},{2,4},{3,5},{4,2},{5,3},{6,0},{7,1},{8,14},{9,15},{10,... | collective-permute-start | bytes 172040 | tf_op jit(solution)/shard_map/ppermute | solution.py:44
  39.9 2.5 %collective-permute-done.15.refs_6_ = bf16[8,3584]{1,0:T(8,128)(2,1)S(1)} collective-permute-done((bf16[8,3584]{1,0:T(8,128)(2,1)S(1)}, bf16[8,3584]{1,0:T(8,128)(2,1)S(1)}, u32[]{:S(2)}, u32[]{:S(2)}) %collective-permute-start.15) | collective-permute-done | bytes 57376 | tf_op jit(solution)/shard_map/ppermute | solution.py:44
  42.4 0.9 %collective-permute-done.16.refs_7_ = bf16[8,3584]{1,0:T(8,128)(2,1)S(1)} collective-permute-done((bf16[8,3584]{1,0:T(8,128)(2,1)S(1)}, bf16[8,3584]{1,0:T(8,128)(2,1)S(1)}, u32[]{:S(2)}, u32[]{:S(2)}) %collective-permute-start.16) | collective-permute-done | bytes 57376 | tf_op jit(solution)/shard_map/ppermute | solution.py:44
  43.2 0.0 collective-permute-done.11.refs_1_
  43.2 0.0 collective-permute-done.12.refs_2_
  43.2 0.0 collective-permute-done.13.refs_3_
  43.3 2.3 %shard_map.130 = (bf16[8,6272]{1,0:T(8,128)(2,1)S(1)}, bf16[8,6272]{1,0:T(8,128)(2,1)S(1)}, bf16[8,6272]{1,0:T(8,128)(2,1)S(1)}, bf16[8,6272]{1,0:T(8,128)(2,1)S(1)}) custom-call(f32[1,3584]{1,0:T(1,128)S(1)} %copy-done.1, bf16[3584,512]{1,0:T(8,128)(2,1)S(1)} %get-tuple-element.85.cols_ref, bf16[256,3584]{1,0:T(8,128)(2,1)S(1)} %get-tuple-element.86.rows_ref, ...), custom_call_target="tpu_custom_call" | custom-call | tf_op jit(solution)/shard_map/pallas_call | solution.py:22
  45.6 1.2 %collective-permute-start.17 = (bf16[8,6272]{1,0:T(8,128)(2,1)S(1)}, bf16[8,6272]{1,0:T(8,128)(2,1)S(1)}, u32[]{:S(2)}, u32[]{:S(2)}) collective-permute-start(bf16[8,6272]{1,0:T(8,128)(2,1)S(1)} %get-tuple-element.121), channel_id=1, source_target_pairs={{0,2},{1,3},{2,0},{3,1},{4,6},{5,7},{6,4},{7,5},{8,10},{9,11},{10,... | collective-permute-start | bytes 301064 | tf_op jit(solution)/shard_map/ppermute | solution.py:44
  46.8 1.1 %collective-permute-start.18 = (bf16[8,6272]{1,0:T(8,128)(2,1)S(1)}, bf16[8,6272]{1,0:T(8,128)(2,1)S(1)}, u32[]{:S(2)}, u32[]{:S(2)}) collective-permute-start(bf16[8,6272]{1,0:T(8,128)(2,1)S(1)} %get-tuple-element.122), channel_id=1, source_target_pairs={{0,4},{1,5},{2,6},{3,7},{4,0},{5,1},{6,2},{7,3},{8,12},{9,13},{10,... | collective-permute-start | bytes 301064 | tf_op jit(solution)/shard_map/ppermute | solution.py:44
  47.9 1.2 %collective-permute-start.19 = (bf16[8,6272]{1,0:T(8,128)(2,1)S(1)}, bf16[8,6272]{1,0:T(8,128)(2,1)S(1)}, u32[]{:S(2)}, u32[]{:S(2)}) collective-permute-start(bf16[8,6272]{1,0:T(8,128)(2,1)S(1)} %get-tuple-element.123), channel_id=1, source_target_pairs={{0,6},{1,7},{2,4},{3,5},{4,2},{5,3},{6,0},{7,1},{8,14},{9,15},{10,... | collective-permute-start | bytes 301064 | tf_op jit(solution)/shard_map/ppermute | solution.py:44
  49.1 1.1 %collective-permute-done.17.refs_1_ = bf16[8,6272]{1,0:T(8,128)(2,1)S(1)} collective-permute-done((bf16[8,6272]{1,0:T(8,128)(2,1)S(1)}, bf16[8,6272]{1,0:T(8,128)(2,1)S(1)}, u32[]{:S(2)}, u32[]{:S(2)}) %collective-permute-start.17) | collective-permute-done | bytes 100384 | tf_op jit(solution)/shard_map/ppermute | solution.py:44
  50.3 1.1 %collective-permute-done.18.refs_2_ = bf16[8,6272]{1,0:T(8,128)(2,1)S(1)} collective-permute-done((bf16[8,6272]{1,0:T(8,128)(2,1)S(1)}, bf16[8,6272]{1,0:T(8,128)(2,1)S(1)}, u32[]{:S(2)}, u32[]{:S(2)}) %collective-permute-start.18) | collective-permute-done | bytes 100384 | tf_op jit(solution)/shard_map/ppermute | solution.py:44
  51.4 2.0 %collective-permute-done.19.refs_3_ = bf16[8,6272]{1,0:T(8,128)(2,1)S(1)} collective-permute-done((bf16[8,6272]{1,0:T(8,128)(2,1)S(1)}, bf16[8,6272]{1,0:T(8,128)(2,1)S(1)}, u32[]{:S(2)}, u32[]{:S(2)}) %collective-permute-start.19) | collective-permute-done | bytes 100384 | tf_op jit(solution)/shard_map/ppermute | solution.py:44
  53.5 0.9 %shard_map.131 = (bf16[24,3584]{1,0:T(8,128)(2,1)}, bf16[24,3584]{1,0:T(8,128)(2,1)}) custom-call(bf16[4,24,32]{2,1,0:T(8,128)(2,1)S(1)} %get-tuple-element.84.tables, bf16[8,6272]{1,0:T(8,128)(2,1)S(1)} %get-tuple-element.120.refs_0_, bf16[8,6272]{1,0:T(8,128)(2,1)S(1)} %collective-permute-done.17.refs_1_, ...), custom_call_target="tpu_custom_call" | custom-call | tf_op jit(solution)/shard_map/pallas_call | solution.py:22
Async XLA Ops:
  0.6 10.8 %copy-start = (bf16[1,2,24,3584]{3,2,1,0:T(8,128)(2,1)S(1)}, bf16[1,2,24,3584]{3,2,1,0:T(8,128)(2,1)}, u32[]{:S(2)}) copy-start(bf16[1,2,24,3584]{3,2,1,0:T(8,128)(2,1)} %param.13) | copy-start | bytes 1032196
  2.2 5.6 %collective-permute-start = (bf16[3584,128]{1,0:T(8,128)(2,1)}, bf16[3584,128]{1,0:T(8,128)(2,1)S(1)}, u32[]{:S(2)}, u32[]{:S(2)}) collective-permute-start(bf16[3584,128]{1,0:T(8,128)(2,1)} %bitcast.14), channel_id=1, source_target_pairs={{0,1},{1,0},{2,3},{3,2},{4,5},{5,4},{6,7},{7,6},{8,9},{9,8},{10,11... | collective-permute-start | bytes 2752520 | tf_op jit(solution)/shard_map/ppermute | solution.py:37
  2.8 9.0 %collective-permute-start.1 = (bf16[3584,128]{1,0:T(8,128)(2,1)}, bf16[3584,128]{1,0:T(8,128)(2,1)S(1)}, u32[]{:S(2)}, u32[]{:S(2)}) collective-permute-start(bf16[3584,128]{1,0:T(8,128)(2,1)} %bitcast.16), channel_id=1, source_target_pairs={{0,1},{1,0},{2,3},{3,2},{4,5},{5,4},{6,7},{7,6},{8,9},{9,8},{10,11... | collective-permute-start | bytes 2752520 | tf_op jit(solution)/shard_map/ppermute | solution.py:37
  2.9 8.9 %collective-permute-start.2 = (bf16[128,3584]{1,0:T(8,128)(2,1)}, bf16[128,3584]{1,0:T(8,128)(2,1)S(1)}, u32[]{:S(2)}, u32[]{:S(2)}) collective-permute-start(bf16[128,3584]{1,0:T(8,128)(2,1)} %bitcast.18), channel_id=1, source_target_pairs={{0,1},{1,0},{2,3},{3,2},{4,5},{5,4},{6,7},{7,6},{8,9},{9,8},{10,11... | collective-permute-start | bytes 2752520 | tf_op jit(solution)/shard_map/ppermute | solution.py:37
  3.7 9.4 %collective-permute-start.3 = (bf16[8,9600]{1,0:T(8,128)(2,1)S(1)}, bf16[8,9600]{1,0:T(8,128)(2,1)S(1)}, u32[]{:S(2)}, u32[]{:S(2)}) collective-permute-start(bf16[8,9600]{1,0:T(8,128)(2,1)S(1)} %get-tuple-element.97), channel_id=1, source_target_pairs={{0,2},{1,3},{2,0},{3,1},{4,6},{5,7},{6,4},{7,5},{8,10},{9,11},{10,... | collective-permute-start | bytes 460808 | tf_op jit(solution)/shard_map/ppermute | solution.py:44
  6.3 9.4 %collective-permute-start.4 = (bf16[8,9600]{1,0:T(8,128)(2,1)S(1)}, bf16[8,9600]{1,0:T(8,128)(2,1)S(1)}, u32[]{:S(2)}, u32[]{:S(2)}) collective-permute-start(bf16[8,9600]{1,0:T(8,128)(2,1)S(1)} %get-tuple-element.98), channel_id=1, source_target_pairs={{0,4},{1,5},{2,6},{3,7},{4,0},{5,1},{6,2},{7,3},{8,12},{9,13},{10,... | collective-permute-start | bytes 460808 | tf_op jit(solution)/shard_map/ppermute | solution.py:44
  7.8 7.8 %collective-permute-start.5 = (bf16[8,9600]{1,0:T(8,128)(2,1)S(1)}, bf16[8,9600]{1,0:T(8,128)(2,1)S(1)}, u32[]{:S(2)}, u32[]{:S(2)}) collective-permute-start(bf16[8,9600]{1,0:T(8,128)(2,1)S(1)} %get-tuple-element.99), channel_id=1, source_target_pairs={{0,6},{1,7},{2,4},{3,5},{4,2},{5,3},{6,0},{7,1},{8,14},{9,15},{10,... | collective-permute-start | bytes 460808 | tf_op jit(solution)/shard_map/ppermute | solution.py:44
  11.8 3.9 %copy-start.1 = (f32[1,3584]{1,0:T(1,128)S(1)}, f32[1,3584]{1,0:T(1,128)}, u32[]{:S(2)}) copy-start(f32[1,3584]{1,0:T(1,128)} %gain_ref.3) | copy-start | bytes 43012
  18.1 5.1 %collective-permute-start.6 = (bf16[8,6272]{1,0:T(8,128)(2,1)S(1)}, bf16[8,6272]{1,0:T(8,128)(2,1)S(1)}, u32[]{:S(2)}, u32[]{:S(2)}) collective-permute-start(bf16[8,6272]{1,0:T(8,128)(2,1)S(1)} %get-tuple-element.101), channel_id=1, source_target_pairs={{0,2},{1,3},{2,0},{3,1},{4,6},{5,7},{6,4},{7,5},{8,10},{9,11},{10,... | collective-permute-start | bytes 301064 | tf_op jit(solution)/shard_map/ppermute | solution.py:44
  19.4 6.5 %collective-permute-start.7 = (bf16[8,6272]{1,0:T(8,128)(2,1)S(1)}, bf16[8,6272]{1,0:T(8,128)(2,1)S(1)}, u32[]{:S(2)}, u32[]{:S(2)}) collective-permute-start(bf16[8,6272]{1,0:T(8,128)(2,1)S(1)} %get-tuple-element.102), channel_id=1, source_target_pairs={{0,4},{1,5},{2,6},{3,7},{4,0},{5,1},{6,2},{7,3},{8,12},{9,13},{10,... | collective-permute-start | bytes 301064 | tf_op jit(solution)/shard_map/ppermute | solution.py:44
  20.2 5.7 %collective-permute-start.8 = (bf16[8,6272]{1,0:T(8,128)(2,1)S(1)}, bf16[8,6272]{1,0:T(8,128)(2,1)S(1)}, u32[]{:S(2)}, u32[]{:S(2)}) collective-permute-start(bf16[8,6272]{1,0:T(8,128)(2,1)S(1)} %get-tuple-element.103), channel_id=1, source_target_pairs={{0,6},{1,7},{2,4},{3,5},{4,2},{5,3},{6,0},{7,1},{8,14},{9,15},{10,... | collective-permute-start | bytes 301064 | tf_op jit(solution)/shard_map/ppermute | solution.py:44
  26.3 4.6 %collective-permute-start.10 = (bf16[24,3584]{1,0:T(8,128)(2,1)S(1)}, bf16[24,3584]{1,0:T(8,128)(2,1)S(1)}, u32[]{:S(2)}, u32[]{:S(2)}) collective-permute-start(bf16[24,3584]{1,0:T(8,128)(2,1)S(1)} %get-tuple-element.111), channel_id=1, source_target_pairs={{0,1},{1,0},{2,3},{3,2},{4,5},{5,4},{6,7},{7,6},{8,16},{9,17},{10,... | collective-permute-start | bytes 516104 | tf_op jit(solution)/shard_map/ppermute | solution.py:55
  26.4 6.8 %collective-permute-start.9 = (bf16[24,3584]{1,0:T(8,128)(2,1)S(1)}, bf16[24,3584]{1,0:T(8,128)(2,1)S(1)}, u32[]{:S(2)}, u32[]{:S(2)}) collective-permute-start(bf16[24,3584]{1,0:T(8,128)(2,1)S(1)} %get-tuple-element.110), channel_id=1, source_target_pairs={{0,8},{1,9},{2,10},{3,11},{4,12},{5,13},{6,14},{7,15},{8,0},{9,1},... | collective-permute-start | bytes 516104 | tf_op jit(solution)/shard_map/ppermute | solution.py:55
  29.4 8.7 %collective-permute-start.14 = (bf16[8,3584]{1,0:T(8,128)(2,1)S(1)}, bf16[8,3584]{1,0:T(8,128)(2,1)S(1)}, u32[]{:S(2)}, u32[]{:S(2)}) collective-permute-start(bf16[8,3584]{1,0:T(8,128)(2,1)S(1)} %get-tuple-element.117), channel_id=1, source_target_pairs={{0,2},{1,3},{2,0},{3,1},{4,6},{5,7},{6,4},{7,5},{8,10},{9,11},{10,... | collective-permute-start | bytes 172040 | tf_op jit(solution)/shard_map/ppermute | solution.py:44
  33.5 9.8 %collective-permute-start.11 = (bf16[8,6400]{1,0:T(8,128)(2,1)S(1)}, bf16[8,6400]{1,0:T(8,128)(2,1)S(1)}, u32[]{:S(2)}, u32[]{:S(2)}) collective-permute-start(bf16[8,6400]{1,0:T(8,128)(2,1)S(1)} %get-tuple-element.113), channel_id=1, source_target_pairs={{0,2},{1,3},{2,0},{3,1},{4,6},{5,7},{6,4},{7,5},{8,10},{9,11},{10,... | collective-permute-start | bytes 307208 | tf_op jit(solution)/shard_map/ppermute | solution.py:44
  34.9 8.3 %collective-permute-start.12 = (bf16[8,6400]{1,0:T(8,128)(2,1)S(1)}, bf16[8,6400]{1,0:T(8,128)(2,1)S(1)}, u32[]{:S(2)}, u32[]{:S(2)}) collective-permute-start(bf16[8,6400]{1,0:T(8,128)(2,1)S(1)} %get-tuple-element.114), channel_id=1, source_target_pairs={{0,4},{1,5},{2,6},{3,7},{4,0},{5,1},{6,2},{7,3},{8,12},{9,13},{10,... | collective-permute-start | bytes 307208 | tf_op jit(solution)/shard_map/ppermute | solution.py:44
  35.8 7.5 %collective-permute-start.13 = (bf16[8,6400]{1,0:T(8,128)(2,1)S(1)}, bf16[8,6400]{1,0:T(8,128)(2,1)S(1)}, u32[]{:S(2)}, u32[]{:S(2)}) collective-permute-start(bf16[8,6400]{1,0:T(8,128)(2,1)S(1)} %get-tuple-element.115), channel_id=1, source_target_pairs={{0,6},{1,7},{2,4},{3,5},{4,2},{5,3},{6,0},{7,1},{8,14},{9,15},{10,... | collective-permute-start | bytes 307208 | tf_op jit(solution)/shard_map/ppermute | solution.py:44
  37.0 5.4 %collective-permute-start.15 = (bf16[8,3584]{1,0:T(8,128)(2,1)S(1)}, bf16[8,3584]{1,0:T(8,128)(2,1)S(1)}, u32[]{:S(2)}, u32[]{:S(2)}) collective-permute-start(bf16[8,3584]{1,0:T(8,128)(2,1)S(1)} %get-tuple-element.118), channel_id=1, source_target_pairs={{0,4},{1,5},{2,6},{3,7},{4,0},{5,1},{6,2},{7,3},{8,12},{9,13},{10,... | collective-permute-start | bytes 172040 | tf_op jit(solution)/shard_map/ppermute | solution.py:44
  38.2 5.1 %collective-permute-start.16 = (bf16[8,3584]{1,0:T(8,128)(2,1)S(1)}, bf16[8,3584]{1,0:T(8,128)(2,1)S(1)}, u32[]{:S(2)}, u32[]{:S(2)}) collective-permute-start(bf16[8,3584]{1,0:T(8,128)(2,1)S(1)} %get-tuple-element.119), channel_id=1, source_target_pairs={{0,6},{1,7},{2,4},{3,5},{4,2},{5,3},{6,0},{7,1},{8,14},{9,15},{10,... | collective-permute-start | bytes 172040 | tf_op jit(solution)/shard_map/ppermute | solution.py:44
  45.6 4.7 %collective-permute-start.17 = (bf16[8,6272]{1,0:T(8,128)(2,1)S(1)}, bf16[8,6272]{1,0:T(8,128)(2,1)S(1)}, u32[]{:S(2)}, u32[]{:S(2)}) collective-permute-start(bf16[8,6272]{1,0:T(8,128)(2,1)S(1)} %get-tuple-element.121), channel_id=1, source_target_pairs={{0,2},{1,3},{2,0},{3,1},{4,6},{5,7},{6,4},{7,5},{8,10},{9,11},{10,... | collective-permute-start | bytes 301064 | tf_op jit(solution)/shard_map/ppermute | solution.py:44
  46.8 4.6 %collective-permute-start.18 = (bf16[8,6272]{1,0:T(8,128)(2,1)S(1)}, bf16[8,6272]{1,0:T(8,128)(2,1)S(1)}, u32[]{:S(2)}, u32[]{:S(2)}) collective-permute-start(bf16[8,6272]{1,0:T(8,128)(2,1)S(1)} %get-tuple-element.122), channel_id=1, source_target_pairs={{0,4},{1,5},{2,6},{3,7},{4,0},{5,1},{6,2},{7,3},{8,12},{9,13},{10,... | collective-permute-start | bytes 301064 | tf_op jit(solution)/shard_map/ppermute | solution.py:44
  47.9 5.5 %collective-permute-start.19 = (bf16[8,6272]{1,0:T(8,128)(2,1)S(1)}, bf16[8,6272]{1,0:T(8,128)(2,1)S(1)}, u32[]{:S(2)}, u32[]{:S(2)}) collective-permute-start(bf16[8,6272]{1,0:T(8,128)(2,1)S(1)} %get-tuple-element.123), channel_id=1, source_target_pairs={{0,6},{1,7},{2,4},{3,5},{4,2},{5,3},{6,0},{7,1},{8,14},{9,15},{10,... | collective-permute-start | bytes 301064 | tf_op jit(solution)/shard_map/ppermute | solution.py:44

commit v2 on v1

--- a/solution.py
+++ b/solution.py
@@ -231,14 +231,16 @@
     return (to_tokens, to_slots, gates), later
 
 
-def spread_body(step, tables, gates, low, high, *outs):
+def spread_body(step, begin, tables, gates, low, high, *outs):
     even = lax.axis_index("pipe") % 2 == 0
+    span = slice(begin * SLOT, (begin + len(outs)) * SLOT)
     for m, out in enumerate(outs):
-        out[:, :LANES] = gates[step, m * SLOT : (m + 1) * SLOT, :]
+        out[:, :LANES] = gates[step, (begin + m) * SLOT : (begin + m + 1) * SLOT, :]
 
     def put(forward, backward):
         parts = [
-            placed(tables[2 * step + i], rows[...]) for i, rows in enumerate((forward, backward))
+            placed(tables[2 * step + i][span], rows[...])
+            for i, rows in enumerate((forward, backward))
         ]
         put_folded(outs, LANES, parts)
 
@@ -414,8 +416,11 @@
         high = swap_ranks(made[1], 1)
         low = swap_ranks(made[0], 0)
         ahead = exchange(ahead)
-        body = functools.partial(spread_body, step + 1)
-        made = call(body, main, [to_slots, gates, low, high])
+        args = [to_slots, gates, low, high]
+        body = functools.partial(spread_body, step + 1, EXPERTS - 1)
+        far = call(body, main[:1], args)
+        body = functools.partial(spread_body, step + 1, 0)
+        made = [*call(body, main[1:], args), *far]
         pieces = exchange(made) + ahead
 
 

time: 54.6 us -> 54.9 us (level)
    pallas_call x10 -> x11, Pallas kernels: 12.5 us -> 12.7 us  [call(): pl.pallas_call(body, out_shape=outs, compiler_params=pltpu.CompilerParams...]
where the time goes in v2:
time: 54.9 us; the launch traced here: 54.7 us
  starting transfers between devices  24.4 us (44%)
  waiting for transfers between devices  16.7 us (30%)
  Pallas kernels  12.7 us (23%)
  between operations  0.79 us (1%)
    ppermute x15, starting transfers between devices, exchange(): moved.append(lax.ppermute(pieces[m], 'expert', pairs))  20.2 us
    ppermute x15, waiting for transfers between devices, exchange(): moved.append(lax.ppermute(pieces[m], 'expert', pairs))  14.5 us
    pallas_call x11, Pallas kernels, call(): pl.pallas_call(body, out_shape=outs, compiler_params=pltpu.CompilerParams...  12.7 us
    ppermute x2, starting transfers between devices, swap_ranks(): return lax.ppermute(array, ('pipe', 'expert'), list(enumerate(target)))  3.15 us
    ppermute x2, waiting for transfers between devices, swap_ranks(): return lax.ppermute(array, ('pipe', 'expert'), list(enumerate(target)))  2.27 us
  transfers between devices with their start and end apart: 20, of which 9 were waited for; matrix products, arithmetic and copies ran while one was open for 0% of the time, Pallas kernels for 9%

profile of v2, /device:TPU:0, one launch (start us, length us, event | category | flops | bytes accessed | tf_op | source)
XLA Modules:
  0.0 54.7 jit_solution(3842479572468454225)
XLA Ops:
  0.6 0.0 copy-start
  0.6 1.6 %shard_map.122 = (f32[8,128]{1,0:T(8,128)S(1)}, bf16[24,3584]{1,0:T(8,128)(2,1)S(1)}, bf16[24,3584]{1,0:T(8,128)(2,1)S(1)}, bf16[24,3584]{1,0:T(8,128)(2,1)S(1)}...) custom-call(s32[2,24]{1,0:T(2,128)} %bitcast.22, s32[2,24]{1,0:T(2,128)} %bitcast.23, ...), custom_call_target="tpu_custom_call" | custom-call | tf_op jit(solution)/shard_map/pallas_call | solution.py:22
  2.2 0.6 %collective-permute-start = (bf16[3584,128]{1,0:T(8,128)(2,1)}, bf16[3584,128]{1,0:T(8,128)(2,1)S(1)}, u32[]{:S(2)}, u32[]{:S(2)}) collective-permute-start(bf16[3584,128]{1,0:T(8,128)(2,1)} %bitcast.14), channel_id=1, source_target_pairs={{0,1},{1,0},{2,3},{3,2},{4,5},{5,4},{6,7},{7,6},{8,9},{9,8},{10,11... | collective-permute-start | bytes 2752520 | tf_op jit(solution)/shard_map/ppermute | solution.py:37
  2.8 0.1 collective-permute-start.1
  2.9 0.4 collective-permute-start.2
  3.3 0.4 shard_map.126
  3.7 2.6 %collective-permute-start.3 = (bf16[8,9600]{1,0:T(8,128)(2,1)S(1)}, bf16[8,9600]{1,0:T(8,128)(2,1)S(1)}, u32[]{:S(2)}, u32[]{:S(2)}) collective-permute-start(bf16[8,9600]{1,0:T(8,128)(2,1)S(1)} %get-tuple-element.96), channel_id=1, source_target_pairs={{0,2},{1,3},{2,0},{3,1},{4,6},{5,7},{6,4},{7,5},{8,10},{9,11},{10,... | collective-permute-start | bytes 460808 | tf_op jit(solution)/shard_map/ppermute | solution.py:44
  6.3 1.5 %collective-permute-start.4 = (bf16[8,9600]{1,0:T(8,128)(2,1)S(1)}, bf16[8,9600]{1,0:T(8,128)(2,1)S(1)}, u32[]{:S(2)}, u32[]{:S(2)}) collective-permute-start(bf16[8,9600]{1,0:T(8,128)(2,1)S(1)} %get-tuple-element.97), channel_id=1, source_target_pairs={{0,4},{1,5},{2,6},{3,7},{4,0},{5,1},{6,2},{7,3},{8,12},{9,13},{10,... | collective-permute-start | bytes 460808 | tf_op jit(solution)/shard_map/ppermute | solution.py:44
  7.8 0.0 collective-permute-done.refs_0_
  7.8 1.1 %collective-permute-start.5 = (bf16[8,9600]{1,0:T(8,128)(2,1)S(1)}, bf16[8,9600]{1,0:T(8,128)(2,1)S(1)}, u32[]{:S(2)}, u32[]{:S(2)}) collective-permute-start(bf16[8,9600]{1,0:T(8,128)(2,1)S(1)} %get-tuple-element.98), channel_id=1, source_target_pairs={{0,6},{1,7},{2,4},{3,5},{4,2},{5,3},{6,0},{7,1},{8,14},{9,15},{10,... | collective-permute-start | bytes 460808 | tf_op jit(solution)/shard_map/ppermute | solution.py:44
  8.9 2.5 %shard_map.123 = (bf16[3584,512]{1,0:T(8,128)(2,1)S(1)}, bf16[256,3584]{1,0:T(8,128)(2,1)S(1)}, bf16[512,3584]{1,0:T(8,128)(2,1)S(1)}, bf16[3584,256]{1,0:T(8,128)(2,1)S(1)}) custom-call(bf16[3584,128]{1,0:T(8,128)(2,1)} %bitcast.15, bf16[3584,128]{1,0:T(8,128)(2,1)} %bitcast.17, bf16[128,3584]{1,0:T(8,128)(2,1)} %bitcast.19), custom_call_target="tpu_custom_call" | custom-call | tf_op jit(solution)/shard_map/pallas_call | solution.py:22
  11.4 0.0 copy-done
  11.4 0.3 shard_map.125
  11.8 0.0 collective-permute-done.1.refs_1_
  11.8 0.0 collective-permute-done.2.refs_2_
  11.8 0.0 copy-start.1
  11.8 1.3 %shard_map.124 = (bf16[3584,512]{1,0:T(8,128)(2,1)S(1)}, bf16[256,3584]{1,0:T(8,128)(2,1)S(1)}, bf16[512,3584]{1,0:T(8,128)(2,1)S(1)}, bf16[3584,256]{1,0:T(8,128)(2,1)S(1)}) custom-call(bf16[3584,128]{1,0:T(8,128)(2,1)S(1)} %collective-permute-done.refs_0_, ...), custom_call_target="tpu_custom_call", output_to_operand_aliasing={{0}: (3, {}), {1}: (4, {}), {2}: (5, {}), {3}: (6, {})} | custom-call | tf_op jit(solution)/shard_map/pallas_call | solution.py:22
  13.1 0.0 collective-permute-done.3.refs_1_
  13.1 2.6 %collective-permute-done.4.refs_2_ = bf16[8,9600]{1,0:T(8,128)(2,1)S(1)} collective-permute-done((bf16[8,9600]{1,0:T(8,128)(2,1)S(1)}, bf16[8,9600]{1,0:T(8,128)(2,1)S(1)}, u32[]{:S(2)}, u32[]{:S(2)}) %collective-permute-start.4) | collective-permute-done | bytes 153632 | tf_op jit(solution)/shard_map/ppermute | solution.py:44
  15.7 0.0 collective-permute-done.5.refs_3_
  15.7 0.0 copy-done.1
  15.7 2.5 %shard_map.127 = (bf16[8,6272]{1,0:T(8,128)(2,1)S(1)}, bf16[8,6272]{1,0:T(8,128)(2,1)S(1)}, bf16[8,6272]{1,0:T(8,128)(2,1)S(1)}, bf16[8,6272]{1,0:T(8,128)(2,1)S(1)}) custom-call(f32[1,3584]{1,0:T(1,128)S(1)} %copy-done.1, bf16[3584,512]{1,0:T(8,128)(2,1)S(1)} %get-tuple-element.84.cols_ref, bf16[256,3584]{1,0:T(8,128)(2,1)S(1)} %get-tuple-element.85.rows_ref, ...), custom_call_target="tpu_custom_call" | custom-call | tf_op jit(solution)/shard_map/pallas_call | solution.py:22
  18.1 1.3 %collective-permute-start.6 = (bf16[8,6272]{1,0:T(8,128)(2,1)S(1)}, bf16[8,6272]{1,0:T(8,128)(2,1)S(1)}, u32[]{:S(2)}, u32[]{:S(2)}) collective-permute-start(bf16[8,6272]{1,0:T(8,128)(2,1)S(1)} %get-tuple-element.100), channel_id=1, source_target_pairs={{0,2},{1,3},{2,0},{3,1},{4,6},{5,7},{6,4},{7,5},{8,10},{9,11},{10,... | collective-permute-start | bytes 301064 | tf_op jit(solution)/shard_map/ppermute | solution.py:44
  19.4 0.8 %collective-permute-start.7 = (bf16[8,6272]{1,0:T(8,128)(2,1)S(1)}, bf16[8,6272]{1,0:T(8,128)(2,1)S(1)}, u32[]{:S(2)}, u32[]{:S(2)}) collective-permute-start(bf16[8,6272]{1,0:T(8,128)(2,1)S(1)} %get-tuple-element.101), channel_id=1, source_target_pairs={{0,4},{1,5},{2,6},{3,7},{4,0},{5,1},{6,2},{7,3},{8,12},{9,13},{10,... | collective-permute-start | bytes 301064 | tf_op jit(solution)/shard_map/ppermute | solution.py:44
  20.2 1.5 %collective-permute-start.8 = (bf16[8,6272]{1,0:T(8,128)(2,1)S(1)}, bf16[8,6272]{1,0:T(8,128)(2,1)S(1)}, u32[]{:S(2)}, u32[]{:S(2)}) collective-permute-start(bf16[8,6272]{1,0:T(8,128)(2,1)S(1)} %get-tuple-element.102), channel_id=1, source_target_pairs={{0,6},{1,7},{2,4},{3,5},{4,2},{5,3},{6,0},{7,1},{8,14},{9,15},{10,... | collective-permute-start | bytes 301064 | tf_op jit(solution)/shard_map/ppermute | solution.py:44
  21.7 1.5 %collective-permute-done.6.refs_1_ = bf16[8,6272]{1,0:T(8,128)(2,1)S(1)} collective-permute-done((bf16[8,6272]{1,0:T(8,128)(2,1)S(1)}, bf16[8,6272]{1,0:T(8,128)(2,1)S(1)}, u32[]{:S(2)}, u32[]{:S(2)}) %collective-permute-start.6) | collective-permute-done | bytes 100384 | tf_op jit(solution)/shard_map/ppermute | solution.py:44
  23.2 2.7 %collective-permute-done.7.refs_2_ = bf16[8,6272]{1,0:T(8,128)(2,1)S(1)} collective-permute-done((bf16[8,6272]{1,0:T(8,128)(2,1)S(1)}, bf16[8,6272]{1,0:T(8,128)(2,1)S(1)}, u32[]{:S(2)}, u32[]{:S(2)}) %collective-permute-start.7) | collective-permute-done | bytes 100384 | tf_op jit(solution)/shard_map/ppermute | solution.py:44
  25.9 0.0 collective-permute-done.8.refs_3_
  25.9 0.4 shard_map.128
  26.3 0.1 collective-permute-start.10
  26.4 3.1 %collective-permute-start.9 = (bf16[24,3584]{1,0:T(8,128)(2,1)S(1)}, bf16[24,3584]{1,0:T(8,128)(2,1)S(1)}, u32[]{:S(2)}, u32[]{:S(2)}) collective-permute-start(bf16[24,3584]{1,0:T(8,128)(2,1)S(1)} %get-tuple-element.109), channel_id=1, source_target_pairs={{0,8},{1,9},{2,10},{3,11},{4,12},{5,13},{6,14},{7,15},{8,0},{9,1},... | collective-permute-start | bytes 516104 | tf_op jit(solution)/shard_map/ppermute | solution.py:55
  29.4 1.4 %collective-permute-start.14 = (bf16[8,3584]{1,0:T(8,128)(2,1)S(1)}, bf16[8,3584]{1,0:T(8,128)(2,1)S(1)}, u32[]{:S(2)}, u32[]{:S(2)}) collective-permute-start(bf16[8,3584]{1,0:T(8,128)(2,1)S(1)} %get-tuple-element.115), channel_id=1, source_target_pairs={{0,2},{1,3},{2,0},{3,1},{4,6},{5,7},{6,4},{7,5},{8,10},{9,11},{10,... | collective-permute-start | bytes 172040 | tf_op jit(solution)/shard_map/ppermute | solution.py:44
  30.9 0.0 collective-permute-done.10.high
  30.9 2.3 %collective-permute-done.9.low = bf16[24,3584]{1,0:T(8,128)(2,1)S(1)} collective-permute-done((bf16[24,3584]{1,0:T(8,128)(2,1)S(1)}, bf16[24,3584]{1,0:T(8,128)(2,1)S(1)}, u32[]{:S(2)}, u32[]{:S(2)}) %collective-permute-start.9) | collective-permute-done | bytes 172064 | tf_op jit(solution)/shard_map/ppermute | solution.py:55
  33.2 0.2 shard_map.130
  33.4 1.7 %collective-permute-start.13 = (bf16[8,6400]{1,0:T(8,128)(2,1)S(1)}, bf16[8,6400]{1,0:T(8,128)(2,1)S(1)}, u32[]{:S(2)}, u32[]{:S(2)}) collective-permute-start(bf16[8,6400]{1,0:T(8,128)(2,1)S(1)} %shard_map.130), channel_id=1, source_target_pairs={{0,6},{1,7},{2,4},{3,5},{4,2},{5,3},{6,0},{7,1},{8,14},{9,15},{10,... | collective-permute-start | bytes 307208 | tf_op jit(solution)/shard_map/ppermute | solution.py:44
  35.1 0.3 shard_map.129
  35.4 1.0 %collective-permute-start.11 = (bf16[8,6400]{1,0:T(8,128)(2,1)S(1)}, bf16[8,6400]{1,0:T(8,128)(2,1)S(1)}, u32[]{:S(2)}, u32[]{:S(2)}) collective-permute-start(bf16[8,6400]{1,0:T(8,128)(2,1)S(1)} %get-tuple-element.112), channel_id=1, source_target_pairs={{0,2},{1,3},{2,0},{3,1},{4,6},{5,7},{6,4},{7,5},{8,10},{9,11},{10,... | collective-permute-start | bytes 307208 | tf_op jit(solution)/shard_map/ppermute | solution.py:44
  36.4 0.9 %collective-permute-start.12 = (bf16[8,6400]{1,0:T(8,128)(2,1)S(1)}, bf16[8,6400]{1,0:T(8,128)(2,1)S(1)}, u32[]{:S(2)}, u32[]{:S(2)}) collective-permute-start(bf16[8,6400]{1,0:T(8,128)(2,1)S(1)} %get-tuple-element.113), channel_id=1, source_target_pairs={{0,4},{1,5},{2,6},{3,7},{4,0},{5,1},{6,2},{7,3},{8,12},{9,13},{10,... | collective-permute-start | bytes 307208 | tf_op jit(solution)/shard_map/ppermute | solution.py:44
  37.3 1.1 %collective-permute-start.15 = (bf16[8,3584]{1,0:T(8,128)(2,1)S(1)}, bf16[8,3584]{1,0:T(8,128)(2,1)S(1)}, u32[]{:S(2)}, u32[]{:S(2)}) collective-permute-start(bf16[8,3584]{1,0:T(8,128)(2,1)S(1)} %get-tuple-element.116), channel_id=1, source_target_pairs={{0,4},{1,5},{2,6},{3,7},{4,0},{5,1},{6,2},{7,3},{8,12},{9,13},{10,... | collective-permute-start | bytes 172040 | tf_op jit(solution)/shard_map/ppermute | solution.py:44
  38.4 0.0 collective-permute-done.14.refs_5_
  38.4 1.7 %collective-permute-start.16 = (bf16[8,3584]{1,0:T(8,128)(2,1)S(1)}, bf16[8,3584]{1,0:T(8,128)(2,1)S(1)}, u32[]{:S(2)}, u32[]{:S(2)}) collective-permute-start(bf16[8,3584]{1,0:T(8,128)(2,1)S(1)} %get-tuple-element.117), channel_id=1, source_target_pairs={{0,6},{1,7},{2,4},{3,5},{4,2},{5,3},{6,0},{7,1},{8,14},{9,15},{10,... | collective-permute-start | bytes 172040 | tf_op jit(solution)/shard_map/ppermute | solution.py:44
  40.1 2.0 %collective-permute-done.15.refs_6_ = bf16[8,3584]{1,0:T(8,128)(2,1)S(1)} collective-permute-done((bf16[8,3584]{1,0:T(8,128)(2,1)S(1)}, bf16[8,3584]{1,0:T(8,128)(2,1)S(1)}, u32[]{:S(2)}, u32[]{:S(2)}) %collective-permute-start.15) | collective-permute-done | bytes 57376 | tf_op jit(solution)/shard_map/ppermute | solution.py:44
  42.1 1.4 %collective-permute-done.16.refs_7_ = bf16[8,3584]{1,0:T(8,128)(2,1)S(1)} collective-permute-done((bf16[8,3584]{1,0:T(8,128)(2,1)S(1)}, bf16[8,3584]{1,0:T(8,128)(2,1)S(1)}, u32[]{:S(2)}, u32[]{:S(2)}) %collective-permute-start.16) | collective-permute-done | bytes 57376 | tf_op jit(solution)/shard_map/ppermute | solution.py:44
  43.5 0.0 collective-permute-done.13.refs_3_
  43.5 0.0 collective-permute-done.11.refs_1_
  43.5 0.0 collective-permute-done.12.refs_2_
  43.5 2.3 %shard_map.131 = (bf16[8,6272]{1,0:T(8,128)(2,1)S(1)}, bf16[8,6272]{1,0:T(8,128)(2,1)S(1)}, bf16[8,6272]{1,0:T(8,128)(2,1)S(1)}, bf16[8,6272]{1,0:T(8,128)(2,1)S(1)}) custom-call(f32[1,3584]{1,0:T(1,128)S(1)} %copy-done.1, bf16[3584,512]{1,0:T(8,128)(2,1)S(1)} %get-tuple-element.84.cols_ref, bf16[256,3584]{1,0:T(8,128)(2,1)S(1)} %get-tuple-element.85.rows_ref, ...), custom_call_target="tpu_custom_call" | custom-call | tf_op jit(solution)/shard_map/pallas_call | solution.py:22
  45.9 1.2 %collective-permute-start.17 = (bf16[8,6272]{1,0:T(8,128)(2,1)S(1)}, bf16[8,6272]{1,0:T(8,128)(2,1)S(1)}, u32[]{:S(2)}, u32[]{:S(2)}) collective-permute-start(bf16[8,6272]{1,0:T(8,128)(2,1)S(1)} %get-tuple-element.119), channel_id=1, source_target_pairs={{0,2},{1,3},{2,0},{3,1},{4,6},{5,7},{6,4},{7,5},{8,10},{9,11},{10,... | collective-permute-start | bytes 301064 | tf_op jit(solution)/shard_map/ppermute | solution.py:44
  47.0 1.2 %collective-permute-start.18 = (bf16[8,6272]{1,0:T(8,128)(2,1)S(1)}, bf16[8,6272]{1,0:T(8,128)(2,1)S(1)}, u32[]{:S(2)}, u32[]{:S(2)}) collective-permute-start(bf16[8,6272]{1,0:T(8,128)(2,1)S(1)} %get-tuple-element.120), channel_id=1, source_target_pairs={{0,4},{1,5},{2,6},{3,7},{4,0},{5,1},{6,2},{7,3},{8,12},{9,13},{10,... | collective-permute-start | bytes 301064 | tf_op jit(solution)/shard_map/ppermute | solution.py:44
  48.2 1.2 %collective-permute-start.19 = (bf16[8,6272]{1,0:T(8,128)(2,1)S(1)}, bf16[8,6272]{1,0:T(8,128)(2,1)S(1)}, u32[]{:S(2)}, u32[]{:S(2)}) collective-permute-start(bf16[8,6272]{1,0:T(8,128)(2,1)S(1)} %get-tuple-element.121), channel_id=1, source_target_pairs={{0,6},{1,7},{2,4},{3,5},{4,2},{5,3},{6,0},{7,1},{8,14},{9,15},{10,... | collective-permute-start | bytes 301064 | tf_op jit(solution)/shard_map/ppermute | solution.py:44
  49.4 1.1 %collective-permute-done.17.refs_1_ = bf16[8,6272]{1,0:T(8,128)(2,1)S(1)} collective-permute-done((bf16[8,6272]{1,0:T(8,128)(2,1)S(1)}, bf16[8,6272]{1,0:T(8,128)(2,1)S(1)}, u32[]{:S(2)}, u32[]{:S(2)}) %collective-permute-start.17) | collective-permute-done | bytes 100384 | tf_op jit(solution)/shard_map/ppermute | solution.py:44
  50.6 1.1 %collective-permute-done.18.refs_2_ = bf16[8,6272]{1,0:T(8,128)(2,1)S(1)} collective-permute-done((bf16[8,6272]{1,0:T(8,128)(2,1)S(1)}, bf16[8,6272]{1,0:T(8,128)(2,1)S(1)}, u32[]{:S(2)}, u32[]{:S(2)}) %collective-permute-start.18) | collective-permute-done | bytes 100384 | tf_op jit(solution)/shard_map/ppermute | solution.py:44
  51.7 2.1 %collective-permute-done.19.refs_3_ = bf16[8,6272]{1,0:T(8,128)(2,1)S(1)} collective-permute-done((bf16[8,6272]{1,0:T(8,128)(2,1)S(1)}, bf16[8,6272]{1,0:T(8,128)(2,1)S(1)}, u32[]{:S(2)}, u32[]{:S(2)}) %collective-permute-start.19) | collective-permute-done | bytes 100384 | tf_op jit(solution)/shard_map/ppermute | solution.py:44
  53.7 1.0 %shard_map.132 = (bf16[24,3584]{1,0:T(8,128)(2,1)}, bf16[24,3584]{1,0:T(8,128)(2,1)}) custom-call(bf16[4,24,32]{2,1,0:T(8,128)(2,1)S(1)} %get-tuple-element.83.tables, bf16[8,6272]{1,0:T(8,128)(2,1)S(1)} %get-tuple-element.118.refs_0_, bf16[8,6272]{1,0:T(8,128)(2,1)S(1)} %collective-permute-done.17.refs_1_, ...), custom_call_target="tpu_custom_call" | custom-call | tf_op jit(solution)/shard_map/pallas_call | solution.py:22
Async XLA Ops:
  0.6 10.8 %copy-start = (bf16[1,2,24,3584]{3,2,1,0:T(8,128)(2,1)S(1)}, bf16[1,2,24,3584]{3,2,1,0:T(8,128)(2,1)}, u32[]{:S(2)}) copy-start(bf16[1,2,24,3584]{3,2,1,0:T(8,128)(2,1)} %param.13) | copy-start | bytes 1032196
  2.2 5.6 %collective-permute-start = (bf16[3584,128]{1,0:T(8,128)(2,1)}, bf16[3584,128]{1,0:T(8,128)(2,1)S(1)}, u32[]{:S(2)}, u32[]{:S(2)}) collective-permute-start(bf16[3584,128]{1,0:T(8,128)(2,1)} %bitcast.14), channel_id=1, source_target_pairs={{0,1},{1,0},{2,3},{3,2},{4,5},{5,4},{6,7},{7,6},{8,9},{9,8},{10,11... | collective-permute-start | bytes 2752520 | tf_op jit(solution)/shard_map/ppermute | solution.py:37
  2.8 9.0 %collective-permute-start.1 = (bf16[3584,128]{1,0:T(8,128)(2,1)}, bf16[3584,128]{1,0:T(8,128)(2,1)S(1)}, u32[]{:S(2)}, u32[]{:S(2)}) collective-permute-start(bf16[3584,128]{1,0:T(8,128)(2,1)} %bitcast.16), channel_id=1, source_target_pairs={{0,1},{1,0},{2,3},{3,2},{4,5},{5,4},{6,7},{7,6},{8,9},{9,8},{10,11... | collective-permute-start | bytes 2752520 | tf_op jit(solution)/shard_map/ppermute | solution.py:37
  2.9 8.9 %collective-permute-start.2 = (bf16[128,3584]{1,0:T(8,128)(2,1)}, bf16[128,3584]{1,0:T(8,128)(2,1)S(1)}, u32[]{:S(2)}, u32[]{:S(2)}) collective-permute-start(bf16[128,3584]{1,0:T(8,128)(2,1)} %bitcast.18), channel_id=1, source_target_pairs={{0,1},{1,0},{2,3},{3,2},{4,5},{5,4},{6,7},{7,6},{8,9},{9,8},{10,11... | collective-permute-start | bytes 2752520 | tf_op jit(solution)/shard_map/ppermute | solution.py:37
  3.7 9.4 %collective-permute-start.3 = (bf16[8,9600]{1,0:T(8,128)(2,1)S(1)}, bf16[8,9600]{1,0:T(8,128)(2,1)S(1)}, u32[]{:S(2)}, u32[]{:S(2)}) collective-permute-start(bf16[8,9600]{1,0:T(8,128)(2,1)S(1)} %get-tuple-element.96), channel_id=1, source_target_pairs={{0,2},{1,3},{2,0},{3,1},{4,6},{5,7},{6,4},{7,5},{8,10},{9,11},{10,... | collective-permute-start | bytes 460808 | tf_op jit(solution)/shard_map/ppermute | solution.py:44
  6.3 9.4 %collective-permute-start.4 = (bf16[8,9600]{1,0:T(8,128)(2,1)S(1)}, bf16[8,9600]{1,0:T(8,128)(2,1)S(1)}, u32[]{:S(2)}, u32[]{:S(2)}) collective-permute-start(bf16[8,9600]{1,0:T(8,128)(2,1)S(1)} %get-tuple-element.97), channel_id=1, source_target_pairs={{0,4},{1,5},{2,6},{3,7},{4,0},{5,1},{6,2},{7,3},{8,12},{9,13},{10,... | collective-permute-start | bytes 460808 | tf_op jit(solution)/shard_map/ppermute | solution.py:44
  7.8 7.8 %collective-permute-start.5 = (bf16[8,9600]{1,0:T(8,128)(2,1)S(1)}, bf16[8,9600]{1,0:T(8,128)(2,1)S(1)}, u32[]{:S(2)}, u32[]{:S(2)}) collective-permute-start(bf16[8,9600]{1,0:T(8,128)(2,1)S(1)} %get-tuple-element.98), channel_id=1, source_target_pairs={{0,6},{1,7},{2,4},{3,5},{4,2},{5,3},{6,0},{7,1},{8,14},{9,15},{10,... | collective-permute-start | bytes 460808 | tf_op jit(solution)/shard_map/ppermute | solution.py:44
  11.8 3.9 %copy-start.1 = (f32[1,3584]{1,0:T(1,128)S(1)}, f32[1,3584]{1,0:T(1,128)}, u32[]{:S(2)}) copy-start(f32[1,3584]{1,0:T(1,128)} %gain_ref.3) | copy-start | bytes 43012
  18.1 5.1 %collective-permute-start.6 = (bf16[8,6272]{1,0:T(8,128)(2,1)S(1)}, bf16[8,6272]{1,0:T(8,128)(2,1)S(1)}, u32[]{:S(2)}, u32[]{:S(2)}) collective-permute-start(bf16[8,6272]{1,0:T(8,128)(2,1)S(1)} %get-tuple-element.100), channel_id=1, source_target_pairs={{0,2},{1,3},{2,0},{3,1},{4,6},{5,7},{6,4},{7,5},{8,10},{9,11},{10,... | collective-permute-start | bytes 301064 | tf_op jit(solution)/shard_map/ppermute | solution.py:44
  19.4 6.5 %collective-permute-start.7 = (bf16[8,6272]{1,0:T(8,128)(2,1)S(1)}, bf16[8,6272]{1,0:T(8,128)(2,1)S(1)}, u32[]{:S(2)}, u32[]{:S(2)}) collective-permute-start(bf16[8,6272]{1,0:T(8,128)(2,1)S(1)} %get-tuple-element.101), channel_id=1, source_target_pairs={{0,4},{1,5},{2,6},{3,7},{4,0},{5,1},{6,2},{7,3},{8,12},{9,13},{10,... | collective-permute-start | bytes 301064 | tf_op jit(solution)/shard_map/ppermute | solution.py:44
  20.2 5.7 %collective-permute-start.8 = (bf16[8,6272]{1,0:T(8,128)(2,1)S(1)}, bf16[8,6272]{1,0:T(8,128)(2,1)S(1)}, u32[]{:S(2)}, u32[]{:S(2)}) collective-permute-start(bf16[8,6272]{1,0:T(8,128)(2,1)S(1)} %get-tuple-element.102), channel_id=1, source_target_pairs={{0,6},{1,7},{2,4},{3,5},{4,2},{5,3},{6,0},{7,1},{8,14},{9,15},{10,... | collective-permute-start | bytes 301064 | tf_op jit(solution)/shard_map/ppermute | solution.py:44
  26.3 4.6 %collective-permute-start.10 = (bf16[24,3584]{1,0:T(8,128)(2,1)S(1)}, bf16[24,3584]{1,0:T(8,128)(2,1)S(1)}, u32[]{:S(2)}, u32[]{:S(2)}) collective-permute-start(bf16[24,3584]{1,0:T(8,128)(2,1)S(1)} %get-tuple-element.110), channel_id=1, source_target_pairs={{0,1},{1,0},{2,3},{3,2},{4,5},{5,4},{6,7},{7,6},{8,16},{9,17},{10,... | collective-permute-start | bytes 516104 | tf_op jit(solution)/shard_map/ppermute | solution.py:55
  26.4 6.8 %collective-permute-start.9 = (bf16[24,3584]{1,0:T(8,128)(2,1)S(1)}, bf16[24,3584]{1,0:T(8,128)(2,1)S(1)}, u32[]{:S(2)}, u32[]{:S(2)}) collective-permute-start(bf16[24,3584]{1,0:T(8,128)(2,1)S(1)} %get-tuple-element.109), channel_id=1, source_target_pairs={{0,8},{1,9},{2,10},{3,11},{4,12},{5,13},{6,14},{7,15},{8,0},{9,1},... | collective-permute-start | bytes 516104 | tf_op jit(solution)/shard_map/ppermute | solution.py:55
  29.4 9.0 %collective-permute-start.14 = (bf16[8,3584]{1,0:T(8,128)(2,1)S(1)}, bf16[8,3584]{1,0:T(8,128)(2,1)S(1)}, u32[]{:S(2)}, u32[]{:S(2)}) collective-permute-start(bf16[8,3584]{1,0:T(8,128)(2,1)S(1)} %get-tuple-element.115), channel_id=1, source_target_pairs={{0,2},{1,3},{2,0},{3,1},{4,6},{5,7},{6,4},{7,5},{8,10},{9,11},{10,... | collective-permute-start | bytes 172040 | tf_op jit(solution)/shard_map/ppermute | solution.py:44
  33.4 10.1 %collective-permute-start.13 = (bf16[8,6400]{1,0:T(8,128)(2,1)S(1)}, bf16[8,6400]{1,0:T(8,128)(2,1)S(1)}, u32[]{:S(2)}, u32[]{:S(2)}) collective-permute-start(bf16[8,6400]{1,0:T(8,128)(2,1)S(1)} %shard_map.130), channel_id=1, source_target_pairs={{0,6},{1,7},{2,4},{3,5},{4,2},{5,3},{6,0},{7,1},{8,14},{9,15},{10,... | collective-permute-start | bytes 307208 | tf_op jit(solution)/shard_map/ppermute | solution.py:44
  35.4 8.1 %collective-permute-start.11 = (bf16[8,6400]{1,0:T(8,128)(2,1)S(1)}, bf16[8,6400]{1,0:T(8,128)(2,1)S(1)}, u32[]{:S(2)}, u32[]{:S(2)}) collective-permute-start(bf16[8,6400]{1,0:T(8,128)(2,1)S(1)} %get-tuple-element.112), channel_id=1, source_target_pairs={{0,2},{1,3},{2,0},{3,1},{4,6},{5,7},{6,4},{7,5},{8,10},{9,11},{10,... | collective-permute-start | bytes 307208 | tf_op jit(solution)/shard_map/ppermute | solution.py:44
  36.4 7.1 %collective-permute-start.12 = (bf16[8,6400]{1,0:T(8,128)(2,1)S(1)}, bf16[8,6400]{1,0:T(8,128)(2,1)S(1)}, u32[]{:S(2)}, u32[]{:S(2)}) collective-permute-start(bf16[8,6400]{1,0:T(8,128)(2,1)S(1)} %get-tuple-element.113), channel_id=1, source_target_pairs={{0,4},{1,5},{2,6},{3,7},{4,0},{5,1},{6,2},{7,3},{8,12},{9,13},{10,... | collective-permute-start | bytes 307208 | tf_op jit(solution)/shard_map/ppermute | solution.py:44
  37.3 4.8 %collective-permute-start.15 = (bf16[8,3584]{1,0:T(8,128)(2,1)S(1)}, bf16[8,3584]{1,0:T(8,128)(2,1)S(1)}, u32[]{:S(2)}, u32[]{:S(2)}) collective-permute-start(bf16[8,3584]{1,0:T(8,128)(2,1)S(1)} %get-tuple-element.116), channel_id=1, source_target_pairs={{0,4},{1,5},{2,6},{3,7},{4,0},{5,1},{6,2},{7,3},{8,12},{9,13},{10,... | collective-permute-start | bytes 172040 | tf_op jit(solution)/shard_map/ppermute | solution.py:44
  38.4 5.1 %collective-permute-start.16 = (bf16[8,3584]{1,0:T(8,128)(2,1)S(1)}, bf16[8,3584]{1,0:T(8,128)(2,1)S(1)}, u32[]{:S(2)}, u32[]{:S(2)}) collective-permute-start(bf16[8,3584]{1,0:T(8,128)(2,1)S(1)} %get-tuple-element.117), channel_id=1, source_target_pairs={{0,6},{1,7},{2,4},{3,5},{4,2},{5,3},{6,0},{7,1},{8,14},{9,15},{10,... | collective-permute-start | bytes 172040 | tf_op jit(solution)/shard_map/ppermute | solution.py:44
  45.9 4.7 %collective-permute-start.17 = (bf16[8,6272]{1,0:T(8,128)(2,1)S(1)}, bf16[8,6272]{1,0:T(8,128)(2,1)S(1)}, u32[]{:S(2)}, u32[]{:S(2)}) collective-permute-start(bf16[8,6272]{1,0:T(8,128)(2,1)S(1)} %get-tuple-element.119), channel_id=1, source_target_pairs={{0,2},{1,3},{2,0},{3,1},{4,6},{5,7},{6,4},{7,5},{8,10},{9,11},{10,... | collective-permute-start | bytes 301064 | tf_op jit(solution)/shard_map/ppermute | solution.py:44
  47.0 4.6 %collective-permute-start.18 = (bf16[8,6272]{1,0:T(8,128)(2,1)S(1)}, bf16[8,6272]{1,0:T(8,128)(2,1)S(1)}, u32[]{:S(2)}, u32[]{:S(2)}) collective-permute-start(bf16[8,6272]{1,0:T(8,128)(2,1)S(1)} %get-tuple-element.120), channel_id=1, source_target_pairs={{0,4},{1,5},{2,6},{3,7},{4,0},{5,1},{6,2},{7,3},{8,12},{9,13},{10,... | collective-permute-start | bytes 301064 | tf_op jit(solution)/shard_map/ppermute | solution.py:44
  48.2 5.5 %collective-permute-start.19 = (bf16[8,6272]{1,0:T(8,128)(2,1)S(1)}, bf16[8,6272]{1,0:T(8,128)(2,1)S(1)}, u32[]{:S(2)}, u32[]{:S(2)}) collective-permute-start(bf16[8,6272]{1,0:T(8,128)(2,1)S(1)} %get-tuple-element.121), channel_id=1, source_target_pairs={{0,6},{1,7},{2,4},{3,5},{4,2},{5,3},{6,0},{7,1},{8,14},{9,15},{10,... | collective-permute-start | bytes 301064 | tf_op jit(solution)/shard_map/ppermute | solution.py:44
